TPU v7x, 32 devices: a whole 2x2x4 slice. The times are simulated.
32 devices in a mesh: section: 2 (over core), dp: 4 (over y, x), seq: 4 (over z).
Axes of the slice: x: 2, y: 2, z: 4, core: 2. Of those that a mesh axis runs over, the one named last changes fastest.
Arguments:
- inputs: bfloat16 [2, 4, 1024, 1024], P(None, 'dp', 'seq'), may hold values from -16 to 16
- doc_lengths: int32 [2, 4, 4], P(None, 'dp'), may hold values from 1 to 512, 1024 in all within a row
- out_grad: bfloat16 [2, 4, 1024, 1024], P(None, 'dp', 'seq'), may hold values from -6 to 6
- norm_gain: bfloat16 [2, 1024], P('section', ('dp', 'seq')), may hold values from 0.5 to 1.5
- in_weight: bfloat16 [2, 1024, 4096], P('section', ('dp', 'seq')), may hold values from -0.1875 to 0.1875
- conv_weight: bfloat16 [2, 4, 2048], P('section', None, ('dp', 'seq')), may hold values from -3 to 3
- conv_bias: bfloat16 [2, 2048], P('section', ('dp', 'seq')), may hold values from -0.5 to 0.5
- select_weight: bfloat16 [2, 2048, 96], P('section', ('dp', 'seq')), may hold values from -0.125 to 0.125
- step_weight: bfloat16 [2, 64, 2048], P('section', None, ('dp', 'seq')), may hold values from -0.75 to 0.75
- step_bias: bfloat16 [2, 2048], P('section', ('dp', 'seq')), may hold values from -6.875 to -2.296875
- log_decay: bfloat16 [2, 16, 2048], P('section', None, ('dp', 'seq')), may hold values from -4 to 2
- skip_gain: bfloat16 [2, 2048], P('section', ('dp', 'seq')), may hold values from 0.5 to 1.5
- out_weight: bfloat16 [2, 2048, 1024], P('section', ('dp', 'seq')), may hold values from -0.25 to 0.25
Outputs:
- layer_out: float32 [2, 2, 4, 1024, 1024], P('section', None, 'dp', 'seq')
- layer_in_grad: float32 [2, 2, 4, 1024, 1024], P('section', None, 'dp', 'seq')
- grad_norm_gain: float32 [2, 1024], P('section', ('dp', 'seq'))
- grad_in_weight: float32 [2, 1024, 4096], P('section', ('dp', 'seq'))
- grad_conv_weight: float32 [2, 4, 2048], P('section', None, ('dp', 'seq'))
- grad_conv_bias: float32 [2, 2048], P('section', ('dp', 'seq'))
- grad_select_weight: float32 [2, 2048, 96], P('section', ('dp', 'seq'))
- grad_step_weight: float32 [2, 64, 2048], P('section', None, ('dp', 'seq'))
- grad_step_bias: float32 [2, 2048], P('section', ('dp', 'seq'))
- grad_log_decay: float32 [2, 16, 2048], P('section', None, ('dp', 'seq'))
- grad_skip_gain: float32 [2, 2048], P('section', ('dp', 'seq'))
- grad_out_weight: float32 [2, 2048, 1024], P('section', ('dp', 'seq'))
- step_moments: float32 [2, 2, 2048], P('section', None, ('dp', 'seq'))
Inputs may be any that keep to these rules, and one draw needn't show every extreme that they name: `doc_lengths`: each row's 4 document lengths sum to 1024; the longest is exactly 512.
All inputs are finite; a program needn't handle non-finite values.
Results may differ from a plain program's by a relative error of at most 0.013.
Values may be sent and summed in bfloat16 or wider, within the bound.
A program may use at most 768 MiB of HBM per device.

v0:
```python
import functools
import itertools
import math

import jax
import jax.numpy as jnp
from jax import lax
from jax.experimental import pallas as pl
from jax.experimental.pallas import tpu as pltpu
from jax.sharding import PartitionSpec as P

EPS = 1e-05
LOG2E = math.log2(math.e)
LN2 = math.log(2.0)
CUT = 1e30
LANES = 128
CHUNKS = 8
VMEM_LIMIT = 66_000_000
F32 = jnp.float32
BF16 = jnp.bfloat16


def silu_slope(values):
    sigma = jax.nn.sigmoid(values)
    return sigma * (1.0 + values * (1.0 - sigma))


def interleave(rows):
    count = rows.shape[0]
    return rows.reshape(CHUNKS, count // CHUNKS, -1).swapaxes(0, 1).reshape(count, -1)


def in_order(rows):
    count = rows.shape[0]
    return rows.reshape(count // CHUNKS, CHUNKS, -1).swapaxes(0, 1).reshape(count, -1)


def column_params(**kw):
    return pltpu.CompilerParams(
        dimension_semantics=("arbitrary",), vmem_limit_bytes=VMEM_LIMIT, **kw
    )


def cols(rows, width=LANES):
    return pl.BlockSpec((rows, width), lambda j: (0, j))


def whole(*shape):
    return pl.BlockSpec(shape, lambda j: (0,) * len(shape))


def conv_taps(conv_ref, halo_ref, steps, reach):
    width = conv_ref.shape[1]
    own = conv_ref[...].astype(F32).reshape(steps, CHUNKS, width)
    tail = own[steps - reach :]
    moved = pltpu.roll(tail.reshape(reach * CHUNKS, width), 1, 0).reshape(reach, CHUNKS, width)
    first = lax.broadcasted_iota(jnp.int32, moved.shape, 1) == 0
    halo = halo_ref[...].astype(F32)[:, None, :]
    head = jnp.where(first, jnp.broadcast_to(halo, moved.shape), moved)
    return jnp.concatenate([head, own], axis=0)


def mask_of(same_ref, k, width):
    mask = jnp.concatenate([same_ref[k]] * (width // LANES), axis=1)
    return mask.reshape(-1, CHUNKS, width)


def convolve(ext, small_ref, same_ref, steps, reach):
    width = ext.shape[2]
    pre = jnp.broadcast_to(small_ref[reach + 1 : reach + 2, :], (steps * CHUNKS, width))
    pre = pre.reshape(steps, CHUNKS, width)
    for k in range(reach + 1):
        term = small_ref[k : k + 1, :][None] * ext[k : k + steps]
        pre = pre + (term if k == reach else term * mask_of(same_ref, k, ext.shape[2]))
    return pre.reshape(steps * CHUNKS, width)


def lanes_of(pack_ref, start, stop):
    return jnp.concatenate([pack_ref[i, start:stop, :] for i in range(pack_ref.shape[0])], axis=1)


def select_kernel(conv_ref, halo_ref, same_ref, pack_ref, act_ref, out_ref, acc):
    j = pl.program_id(0)
    count, width = conv_ref.shape
    reach = halo_ref.shape[0]
    steps = count // CHUNKS
    small_ref = lanes_of(pack_ref, pack_ref.shape[1] - 16, pack_ref.shape[1]).astype(F32)
    ext = conv_taps(conv_ref, halo_ref, steps, reach)
    pre = convolve(ext, small_ref, same_ref, steps, reach)
    act = (pre * jax.nn.sigmoid(pre)).astype(BF16)
    act_ref[...] = act

    @pl.when(j == 0)
    def _():
        acc[...] = jnp.zeros_like(acc)

    acc[...] += lax.dot_general(
        act, lanes_of(pack_ref, 0, acc.shape[1]), (((1,), (1,)), ((), ())),
        preferred_element_type=F32,
    )
    out_ref[...] = acc[...]


def pack_blocks(pack, width):
    return pl.BlockSpec((width // LANES,) + pack.shape[1:], lambda j: (j, 0, 0))


def select_call(conv_in, halo, same, pack, wide):
    count, inner = conv_in.shape
    width = min(512, inner)
    return pl.pallas_call(
        select_kernel,
        grid=(inner // width,),
        in_specs=[
            cols(count, width),
            cols(halo.shape[0], width),
            whole(*same.shape),
            pack_blocks(pack, width),
        ],
        out_specs=[cols(count, width), whole(count, wide)],
        out_shape=[
            jax.ShapeDtypeStruct((count, inner), BF16),
            jax.ShapeDtypeStruct((count, wide), F32),
        ],
        scratch_shapes=[pltpu.VMEM((count, wide), F32)],
        compiler_params=column_params(),
        name="conv_select",
    )(conv_in, halo, same, pack)


def spread(dst, src_ref, nstate, at):
    for n in range(nstate):
        dst[n] = jnp.broadcast_to(src_ref[:, at + n : at + n + 1], dst.shape[1:])


def chunk_links(ends, sums, rates, backward):
    row = lax.broadcasted_iota(jnp.int32, (CHUNKS, LANES), 0)
    gains = [jnp.exp2(sums * rate) for rate in rates]
    ends = list(ends)
    total = sums
    k = 1
    while k < CHUNKS:
        turn = CHUNKS - k if backward else k
        mask = row < CHUNKS - k if backward else row >= k
        ends = [
            jnp.where(mask, g * pltpu.roll(e, turn, 0) + e, e) for g, e in zip(gains, ends)
        ]
        gains = [jnp.where(mask, g * pltpu.roll(g, turn, 0), g) for g in gains]
        total = jnp.where(mask, pltpu.roll(total, turn, 0) + total, total)
        k *= 2
    turn = CHUNKS - 1 if backward else 1
    mask = row < CHUNKS - 1 if backward else row >= 1
    entering = [jnp.where(mask, pltpu.roll(e, turn, 0), 0.0) for e in ends]
    before = jnp.where(mask, pltpu.roll(total, turn, 0), 0.0)
    last = 0 if backward else CHUNKS - 1
    return entering, [e[last : last + 1] for e in ends], before, total[last : last + 1]


def rates_of(pack_ref, nstate):
    end = pack_ref.shape[1] - 16
    return -jnp.exp(pack_ref[0, end - nstate : end, :].astype(F32)) * LOG2E


def vector_of(pack_ref, row):
    at = pack_ref.shape[1] - 16
    return pack_ref[0, at : at + 16, :].astype(F32)[row : row + 1]


def rate_rows(rate, nstate):
    return [jnp.broadcast_to(rate[n : n + 1, :], (CHUNKS, LANES)) for n in range(nstate)]


def arriving_state(me, totals_ref, sums_ref, lanes, rate, backward):
    devices = totals_ref.shape[0]
    state = jnp.zeros(rate.shape, F32)
    order = range(devices - 1, 0, -1) if backward else range(devices - 1)
    for k in order:
        passed = jnp.exp2(rate * sums_ref[k, :, lanes]) * state
        passed = passed + totals_ref[k, :, lanes].astype(F32)
        state = jnp.where((k > me) if backward else (k < me), passed, state)
    return state


def conv_grad_kernel(
    conv_ref, halo_ref, same_ref, pack_ref, act_ref, dact_ref, dsel_ref,
    gbias_ref, gskip_ref, dconv_ref, tail_ref, spill_ref, gsel_ref, gsmall_ref,
):
    count, width = conv_ref.shape
    reach = halo_ref.shape[0]
    steps = count // CHUNKS
    ext = conv_taps(conv_ref, halo_ref, steps, reach)
    small_ref = lanes_of(pack_ref, pack_ref.shape[1] - 16, pack_ref.shape[1]).astype(F32)
    sel = lanes_of(pack_ref, 0, dsel_ref.shape[1])
    dsel = dsel_ref[...]
    gsel = lax.dot_general(
        dsel, act_ref[...], (((0,), (0,)), ((), ())), preferred_element_type=F32
    )
    dact = dact_ref[...] + jnp.dot(dsel, sel, preferred_element_type=F32)
    dpre = dact * silu_slope(convolve(ext, small_ref, same_ref, steps, reach))
    vectors = [jnp.sum(dpre, axis=0, keepdims=True), gbias_ref[...], gskip_ref[...]]
    dpre = dpre.reshape(steps, CHUNKS, width)
    parts, taps = [], []
    for k in range(reach + 1):
        masked = dpre if k == reach else dpre * mask_of(same_ref, k, width)
        taps.append(
            jnp.sum((masked * ext[k : k + steps]).reshape(count, width), axis=0, keepdims=True)
        )
        parts.append(masked * small_ref[k : k + 1, :][None])
    vectors = jnp.concatenate(taps + vectors + [jnp.zeros((4 - reach, width), F32)], axis=0)
    for i in range(width // LANES):
        gsel_ref[i] = gsel[:, i * LANES : (i + 1) * LANES].astype(gsel_ref.dtype)
        gsmall_ref[i] = vectors[:, i * LANES : (i + 1) * LANES]
    own = parts[reach]
    for k in range(reach):
        back = reach - k
        own = own + jnp.concatenate(
            [parts[k][back:], jnp.zeros((back, CHUNKS, width), F32)], axis=0
        )
    heads = []
    for e in range(reach):
        total = parts[0][e]
        for k in range(1, e + 1):
            total = total + parts[k][e - k]
        heads.append(total)
    head = jnp.stack(heads)
    spill_ref[...] = head[:, 0, :]
    row = lax.broadcasted_iota(jnp.int32, head.shape, 1)
    moved = pltpu.roll(head.reshape(reach * CHUNKS, width), reach * CHUNKS - 1, 0)
    moved = jnp.where(row == CHUNKS - 1, 0.0, moved.reshape(head.shape))
    tail = own[steps - reach :] + moved
    tail_ref[...] = tail[:, CHUNKS - 1, :]
    dconv = jnp.concatenate([own[: steps - reach], tail], axis=0)
    dconv_ref[...] = dconv.reshape(count, width).astype(BF16)


def conv_grad(conv_in, halo, same, pack, act, dact, dsel, gbias, gskip):
    count, inner = act.shape
    width = min(512, inner)
    reach = halo.shape[0]
    wide = dsel.shape[1]
    return pl.pallas_call(
        conv_grad_kernel,
        grid=(inner // width,),
        in_specs=[
            cols(count, width),
            cols(reach, width),
            whole(*same.shape),
            pack_blocks(pack, width),
            cols(count, width),
            cols(count, width),
            whole(count, wide),
            cols(1, width),
            cols(1, width),
        ],
        out_specs=[
            cols(count, width),
            cols(reach, width),
            cols(reach, width),
            pl.BlockSpec((width // LANES, wide, LANES), lambda j: (j, 0, 0)),
            pl.BlockSpec((width // LANES, 8, LANES), lambda j: (j, 0, 0)),
        ],
        out_shape=[
            jax.ShapeDtypeStruct((count, inner), BF16),
            jax.ShapeDtypeStruct((reach, inner), F32),
            jax.ShapeDtypeStruct((reach, inner), F32),
            jax.ShapeDtypeStruct((inner // LANES, wide, LANES), BF16),
            jax.ShapeDtypeStruct((inner // LANES, 8, LANES), F32),
        ],
        compiler_params=column_params(),
        name="conv_grad",
    )(conv_in, halo, same, pack, act, dact, dsel, gbias, gskip)


def shifted(value, axis, steps):
    count = lax.axis_size(axis)
    first, last = (max(0, -steps), min(count, count - steps))
    return lax.ppermute(value, axis, [(source, source + steps) for source in range(first, last)])


MESH = pl.DeviceIdType.MESH


def where_am_i():
    c, d, z = lax.axis_index("section"), lax.axis_index("dp"), lax.axis_index("seq")
    y, x = d // 2, d % 2
    flip_x, flip_y = y * 2 + (1 - x), (1 - y) * 2 + x
    return c, y, x, z, flip_x, flip_y


def peers_of(depth):
    c, y, x, z, flip_x, flip_y = where_am_i()
    peers = [{"section": 1 - c}, {"dp": flip_x}, {"dp": flip_y}]
    return peers + [{"seq": lax.rem(z + o, depth)} for o in range(1, depth)]


def hail(depth):
    barrier = pltpu.get_barrier_semaphore()
    for peer in peers_of(depth):
        pl.semaphore_signal(barrier, inc=1, device_id=peer, device_id_type=MESH)


def await_hails(depth):
    pl.semaphore_wait(pltpu.get_barrier_semaphore(), 2 + depth)


def greet(depth):
    hail(depth)
    await_hails(depth)


def pipeline(stages, count, lags, extras={}):
    for turn in range(count + lags[-1]):
        for lag, stage in zip(lags, stages):
            if 0 <= turn - lag < count:
                stage(turn - lag)
        if turn in extras:
            extras[turn]()


class Gather:
    def __init__(self, depth, layer, width, base, src, out, mine, send, recv, local):
        self.depth, self.layer, self.width, self.base = depth, layer, width, base
        self.src, self.out, self.mine = src, out, mine
        self.send, self.recv, self.local = send, recv, local
        self.count = mine.shape[0]
        c, y, x, z, flip_x, flip_y = where_am_i()
        self.c, self.y, self.x, self.z = c, y, x, z
        self.near = {"dp": (1 - c) * flip_y + c * flip_x}
        self.far = {"dp": (1 - c) * flip_x + c * flip_y}
        self.partner = {"section": 1 - c}

    def cols(self, k, base=0):
        if isinstance(k, int):
            return pl.ds(base + k * self.width, self.width)
        return pl.ds(pl.multiple_of(base + k * self.width, LANES), self.width)

    def remote(self, k, slot, src, dst, peer):
        return pltpu.make_async_remote_copy(
            src_ref=src, dst_ref=dst, send_sem=self.send.at[k, slot], recv_sem=self.recv.at[k, slot],
            device_id=peer, device_id_type=MESH,
        )

    def piece(self, k, at):
        return self.out.at[at[0], at[1], :, self.c, :, self.cols(k)]

    def pieces(self, k, half):
        rows = self.mine.shape[1]
        if not isinstance(self.src, tuple):
            return [(0, self.src.at[pl.ds(half * rows, rows), self.cols(k, self.base)])]
        found, at = [], 0
        for ref in self.src[half]:
            found.append((at, ref))
            at += ref.shape[0]
        return found

    def hand_wait(self, k):
        return self.remote(k, 0, self.mine.at[k], self.mine.at[k], self.partner)

    def keep_wait(self, k):
        return pltpu.make_async_copy(self.mine.at[k], self.mine.at[k], self.local.at[k, 0])

    def line(self, k):
        target = self.out.at[self.y, self.x, self.z, self.c, :, self.cols(k)]
        return [
            self.remote(k, o, self.mine.at[k], target, {"seq": lax.rem(self.z + o, self.depth)})
            for o in range(1, self.depth)
        ]

    def place(self, k):
        target = self.out.at[self.y, self.x, self.z, self.c, :, self.cols(k)]
        return pltpu.make_async_copy(self.mine.at[k], target, self.local.at[k, 1])

    def move(self, k, slot, at, peer):
        return self.remote(k, self.depth + slot, self.piece(k, at), self.piece(k, at), peer)

    def near_copy(self, k):
        return self.move(k, 0, (self.y, self.x), self.near)

    def far_copy(self, k, core):
        at = (slice(None), self.x) if core == 0 else (self.y, slice(None))
        return self.move(k, 1, at, self.far)

    def cross(self, k):
        return self.move(k, 2, (slice(None), slice(None)), self.partner)

    def first(self, k):
        @pl.when(self.c == self.layer)
        def _():
            for at, ref in self.pieces(k, 1 - self.layer):
                there = self.mine.at[k, pl.ds(at, ref.shape[0])]
                self.remote(k, 0, ref, there, self.partner).start()
            for at, ref in self.pieces(k, self.layer):
                here = self.mine.at[k, pl.ds(at, ref.shape[0])]
                pltpu.make_async_copy(ref, here, self.local.at[k, 0]).start()

    def along_z(self, k):
        @pl.when(self.c == self.layer)
        def _():
            self.hand_wait(k).wait_send()
            self.keep_wait(k).wait()

        @pl.when(self.c != self.layer)
        def _():
            self.hand_wait(k).wait_recv()

        for copy in self.line(k):
            copy.start()
        self.place(k).start()

    def along_near(self, k):
        for copy in self.line(k):
            copy.wait_recv()
        self.place(k).wait()
        self.near_copy(k).start()

    def along_far(self, k):
        self.near_copy(k).wait_recv()
        for core in (0, 1):

            @pl.when(self.c == core)
            def _(core=core):
                self.far_copy(k, core).start()

    def across(self, k):
        self.far_copy(k, 0).wait_recv()
        self.cross(k).start()

    def finish(self, k):
        self.cross(k).wait()
        for copy in self.line(k) + [self.near_copy(k), self.far_copy(k, 0)]:
            copy.wait_send()

    def stages(self):
        return [self.along_z, self.along_near, self.along_far, self.across, self.finish]


def gather_scratch(specs, depth):
    scratch = []
    for rows, columns, width, dtype in specs:
        chunks = columns // width
        scratch += [
            pltpu.VMEM((chunks, rows // 2, width), dtype),
            pltpu.SemaphoreType.DMA((chunks, depth + 3)),
            pltpu.SemaphoreType.DMA((chunks, depth + 3)),
            pltpu.SemaphoreType.DMA((chunks, 2)),
        ]
    return scratch


def gather_shape(rows, columns, depth, dtype):
    return jax.ShapeDtypeStruct((2, 2, depth, 2, rows // 2, columns), dtype)


def gather_kernel(tasks, depth, refs_of, relayed, *refs):
    count = len(tasks)
    inputs = 1 + max(i for of in refs_of for i in (sum(of, ()) if isinstance(of, tuple) else (of,)))
    srcs, refs = refs[:inputs], refs[inputs:]
    relay, refs = refs[:relayed], refs[relayed:]
    outs, relays, rest = refs[:count], refs[count : count + relayed], refs[count + relayed :]
    greet(depth)
    work = []
    for i, ((layer, width, base), of) in enumerate(zip(tasks, refs_of)):
        src = tuple([srcs[n] for n in half] for half in of) if isinstance(of, tuple) else srcs[of]
        gather = Gather(depth, layer, width, base, src, outs[i], *rest[4 * i : 4 * i + 4])
        work += [(gather, k) for k in range(gather.count)]
    for gather, k in work:
        gather.first(k)
    if relayed:
        held, sem = rest[4 * count :]
        pltpu.make_async_copy(relay[0], held, sem).start()
    pipeline(
        [lambda i, s=s: work[i][0].stages()[s](work[i][1]) for s in range(5)],
        len(work), (0, 2, 4, 6, 8),
    )
    if relayed:
        pltpu.make_async_copy(relay[0], held, sem).wait()
        last = pltpu.make_async_copy(held, relays[0], sem)
        last.start()
        last.wait()


def gather_rows(sources, refs_of, tasks, shapes, relay, collective):
    depth = lax.axis_size("seq")
    anywhere = pl.BlockSpec(memory_space=pl.ANY)
    dtype = sources[0].dtype
    relay = [] if relay is None else [relay]
    outs = pl.pallas_call(
        functools.partial(gather_kernel, tasks, depth, refs_of, len(relay)),
        in_specs=[anywhere] * (len(sources) + len(relay)),
        out_specs=[anywhere] * (len(tasks) + len(relay)),
        out_shape=[gather_shape(r, w, depth, dtype) for r, w in shapes]
        + [jax.ShapeDtypeStruct(r.shape, r.dtype) for r in relay],
        scratch_shapes=gather_scratch(
            [(r, w, t[1], dtype) for (r, w), t in zip(shapes, tasks)], depth
        )
        + sum([[pltpu.VMEM(r.shape, r.dtype), pltpu.SemaphoreType.DMA] for r in relay], []),
        compiler_params=pltpu.CompilerParams(
            collective_id=collective, has_side_effects=True, vmem_limit_bytes=VMEM_LIMIT
        ),
        name="gather_rows",
    )(*sources, *relay)
    return [flat_rows(out) for out in outs[: len(tasks)]] + list(outs[len(tasks) :])


def flat_rows(out):
    return out.reshape(-1, out.shape[-1])


class Reduce:
    def __init__(self, depth, layer, width, base, src, out, own, core, side, edge, line, done, send, recv, local):
        self.depth, self.layer, self.width, self.src, self.out = depth, layer, width, src, out
        self.base = base
        self.own, self.core, self.side, self.edge, self.line = own, core, side, edge, line
        self.done, self.send, self.recv, self.local = done, send, recv, local
        self.count, self.held = core.shape[0], own.shape[0]
        self.half = own.shape[4]
        c, y, x, z, flip_x, flip_y = where_am_i()
        self.c, self.y, self.x, self.z = c, y, x, z
        self.near = {"dp": (1 - c) * flip_x + c * flip_y}
        self.far = {"dp": (1 - c) * flip_y + c * flip_x}
        self.kept = (1 - c) * y + c * x
        self.partner = {"section": 1 - c}

    def cols(self, k, base=0):
        if isinstance(k, int):
            return pl.ds(base + k * self.width, self.width)
        return pl.ds(pl.multiple_of(base + k * self.width, LANES), self.width)

    def remote(self, k, slot, src, dst, peer):
        return pltpu.make_async_remote_copy(
            src_ref=src, dst_ref=dst, send_sem=self.send.at[k, slot], recv_sem=self.recv.at[k, slot],
            device_id=peer, device_id_type=MESH,
        )

    def pieces(self, k, half):
        if not isinstance(self.src, tuple):
            rows = pl.ds(half * self.half, self.half)
            return [(0, self.half, self.src.at[:, :, :, rows, self.cols(k)])]
        found, at = [], 0
        for ref in self.src[half]:
            found.append((at, ref.shape[3], ref))
            at += ref.shape[3]
        return found

    def hand_wait(self, k):
        return self.remote(k, 0, self.core.at[k], self.core.at[k], self.partner)

    def slot(self, k):
        return k % self.held if isinstance(k, int) else k & (self.held - 1)

    def keep_wait(self, k):
        own = self.own.at[self.slot(k)]
        return pltpu.make_async_copy(own, own, self.local.at[k, 0])

    def side_copy(self, k, core):
        at = (slice(None), 1 - self.x) if core == 0 else (1 - self.y, slice(None))
        return self.remote(k, 1, self.core.at[k, at[0], at[1]], self.side.at[k], self.near)

    def edges(self, k):
        return self.remote(k, 2, self.side.at[k, 1 - self.kept], self.edge.at[k], self.far)

    def lines(self, k):
        copies = []
        for o in range(1, self.depth):
            peer = lax.rem(self.z + o, self.depth)
            copies.append(
                self.remote(k, 2 + o, self.edge.at[k, peer], self.line.at[k, o - 1], {"seq": peer})
            )
        return copies

    def target(self):
        return pl.ds(self.c * self.half, self.half)

    def give(self, k):
        target = self.out.at[self.target(), self.cols(k, self.base)]
        return self.remote(k, 2 + self.depth, self.done.at[k], target, self.partner)

    def take(self, k):
        target = self.out.at[self.target(), self.cols(k, self.base)]
        return pltpu.make_async_copy(self.done.at[k], target, self.local.at[k, 1])

    def to_core(self, k):
        def begin(theirs, ours):
            for at, rows, ref in self.pieces(k, theirs):
                there = self.core.at[k, :, :, :, pl.ds(at, rows)]
                self.remote(k, 0, ref, there, self.partner).start()
            for at, rows, ref in self.pieces(k, ours):
                here = self.own.at[self.slot(k), :, :, :, pl.ds(at, rows)]
                pltpu.make_async_copy(ref, here, self.local.at[k, 0]).start()

        if not isinstance(self.src, tuple):
            begin(1 - self.c, self.c)
            return
        for core in (0, 1):

            @pl.when(self.c == core)
            def _(core=core):
                begin(1 - core, core)

    def to_near(self, k):
        self.hand_wait(k).wait_recv()
        self.keep_wait(k).wait()
        slot = self.slot(k)
        for at in itertools.product(range(2), range(2), range(self.depth)):
            self.core[(k,) + at] = self.core[(k,) + at] + self.own[(slot,) + at]
        for core in (0, 1):

            @pl.when(self.c == core)
            def _(core=core):
                self.side_copy(k, core).start()

    def to_far(self, k):
        self.side_copy(k, 0).wait_recv()
        c = self.c
        for u in range(2):
            a, b = (1 - c) * u + c * self.y, (1 - c) * self.x + c * u
            for e in range(self.depth):
                self.side[k, u, e] = self.side[k, u, e] + self.core[k, a, b, e]
        self.edges(k).start()

    def to_line(self, k):
        self.edges(k).wait_recv()
        for e in range(self.depth):
            self.edge[k, e] = self.edge[k, e] + self.side[k, self.kept, e]
        for copy in self.lines(k):
            copy.start()

    def to_end(self, k):
        for copy in self.lines(k):
            copy.wait_recv()
        total = self.edge[k, self.z].astype(F32)
        for o in range(self.depth - 1):
            total = total + self.line[k, o].astype(F32)
        self.done[k] = total

        @pl.when(self.c == self.layer)
        def _():
            self.take(k).start()

        @pl.when(self.c != self.layer)
        def _():
            self.give(k).start()

    def finish(self, k):
        @pl.when(self.c == self.layer)
        def _():
            self.take(k).wait()
            self.give(k).wait_recv()

        @pl.when(self.c != self.layer)
        def _():
            self.give(k).wait_send()

        for copy in [self.hand_wait(k), self.side_copy(k, 0), self.edges(k)] + self.lines(k):
            copy.wait_send()

    def stages(self):
        return [self.to_core, self.to_near, self.to_far, self.to_line, self.to_end, self.finish]


def reduce_scratch(specs, depth):
    scratch = []
    for rows, columns, width, dtype in specs:
        chunks, block = columns // width, (rows // 2, width)
        scratch += [
            pltpu.VMEM((min(chunks, 2), 2, 2, depth) + block, dtype),
            pltpu.VMEM((chunks, 2, 2, depth) + block, dtype),
            pltpu.VMEM((chunks, 2, depth) + block, dtype),
            pltpu.VMEM((chunks, depth) + block, dtype),
            pltpu.VMEM((chunks, depth - 1) + block, dtype),
            pltpu.VMEM((chunks,) + block, F32),
            pltpu.SemaphoreType.DMA((chunks, depth + 3)),
            pltpu.SemaphoreType.DMA((chunks, depth + 3)),
            pltpu.SemaphoreType.DMA((chunks, 2)),
        ]
    return scratch


def by_chip(value, depth):
    return value.reshape((2, 2, depth) + value.shape[1:])


def pieces_of(source):
    return list(source[0]) + list(source[1]) if isinstance(source, tuple) else [source]


def shard_of(source):
    first = pieces_of(source)[0]
    rows = sum(piece.shape[1] for piece in pieces_of(source))
    return (rows, first.shape[2])


def split_refs(refs, sources):
    found = []
    for numbers in sources:
        if numbers:
            one, two = numbers
            found.append((refs[:one], refs[one : one + two]))
            refs = refs[one + two :]
        else:
            found.append(refs[0])
            refs = refs[1:]
    return found, refs


def counts_of(sources):
    return [tuple(len(half) for half in s) if isinstance(s, tuple) else 0 for s in sources]


def reduce_kernel(tasks, numbers, homes, olds, depth, pairs, *refs):
    values, refs = refs[: 2 * pairs], refs[2 * pairs :]
    srcs, refs = split_refs(refs, numbers)
    refs = refs[olds:]
    placed, refs = refs[:pairs], refs[pairs:]
    outs, (loaded, ordered, load, swap_send, swap_recv, settle), rest = (
        refs[:homes], refs[homes : homes + 6], refs[homes + 6 :],
    )
    c = lax.axis_index("section")
    greet(depth)
    loads = [pltpu.make_async_copy(v, loaded.at[i], load.at[i]) for i, v in enumerate(values)]

    def local(i, src, dst):
        return pltpu.make_async_copy(src, dst, settle.at[i])

    def remote(i, src, dst):
        return pltpu.make_async_remote_copy(
            src_ref=src, dst_ref=dst, send_sem=swap_send.at[i], recv_sem=swap_recv.at[i],
            device_id={"section": 1 - c}, device_id_type=MESH,
        )

    def begin_moves(i, layer):
        for b in range(ordered.shape[1]):
            target = placed[i].at[layer, :, pl.ds(b * LANES, LANES)]
            local(i, ordered.at[2 * i + layer, b], target).start()
            remote(i, ordered.at[2 * i + 1 - layer, b], target).start()

    def end_moves(i, layer):
        local(i, ordered.at[2 * i + layer], ordered.at[2 * i + layer]).wait()
        remote(i, ordered.at[2 * i + 1 - layer], ordered.at[2 * i + 1 - layer]).wait()

    def each_pair(act):
        for layer in (0, 1):

            @pl.when(c == layer)
            def _(layer=layer):
                for i in range(pairs):
                    act(i, layer)

    def put_in_order():
        steps = loaded.shape[1] // CHUNKS
        for copy in loads:
            copy.wait()

        def step(i, _):
            for n in range(2 * pairs):
                rows = loaded[n, pl.ds(pl.multiple_of(i * CHUNKS, CHUNKS), CHUNKS), :]
                for b in range(ordered.shape[1]):
                    columns = rows[:, b * LANES : (b + 1) * LANES]
                    ordered[n, b, pl.ds(i, CHUNKS, stride=steps), :] = columns
            return 0

        lax.fori_loop(0, steps, step, 0)
        each_pair(begin_moves)

    work = []
    for i, (layer, width, home, base) in enumerate(tasks):
        item = Reduce(depth, layer, width, base, srcs[i], outs[home], *rest[9 * i : 9 * i + 9])
        work += [(item, k) for k in range(item.count)]
    for copy in loads:
        copy.start()
    pipeline(
        [lambda i, s=s: work[i][0].stages()[s](work[i][1]) for s in range(5)],
        len(work), (0, 1, 3, 5, 7), {6: put_in_order},
    )
    for item, k in work:
        item.finish(k)
    each_pair(end_moves)


def reduce_rows(values, tasks, homes, results, collective):
    depth = lax.axis_size("seq")
    pairs = len(results) // 2
    anywhere = pl.BlockSpec(memory_space=pl.ANY)
    arrays = [by_chip(piece, depth) for value in values for piece in pieces_of(value)]
    first = len(results) + len(arrays)
    olds = {i: home for i, home in enumerate(homes) if not isinstance(home, tuple)}
    count, model = results[0].shape
    blocks = (model // LANES, count, LANES)
    outs = pl.pallas_call(
        functools.partial(
            reduce_kernel, tasks, counts_of(values), len(homes), len(olds), depth, pairs
        ),
        in_specs=[anywhere] * (first + len(olds)),
        out_specs=[anywhere] * (pairs + len(homes)),
        out_shape=[jax.ShapeDtypeStruct((2, count, model), F32)] * pairs
        + [jax.ShapeDtypeStruct(home if isinstance(home, tuple) else home.shape, F32) for home in homes],
        scratch_shapes=[
            pltpu.VMEM((2 * pairs,) + results[0].shape, F32),
            pltpu.VMEM((2 * pairs,) + blocks, F32),
        ]
        + [pltpu.SemaphoreType.DMA((2 * pairs,))]
        + [pltpu.SemaphoreType.DMA((pairs,))] * 3
        + reduce_scratch([shard_of(v) + (t[1], BF16) for v, t in zip(values, tasks)], depth),
        input_output_aliases={first + n: pairs + i for n, i in enumerate(olds)},
        compiler_params=pltpu.CompilerParams(
            collective_id=collective, has_side_effects=True, vmem_limit_bytes=VMEM_LIMIT
        ),
        name="reduce_rows",
    )(*results, *arrays, *olds.values())
    return outs[:pairs], outs[pairs:]


def scan_map(phases, shift=0):
    def index(p, j, last):
        if phases == 2:
            return shift + j
        if phases == 0:
            return shift + j * (1 - p) + last * p
        return shift + j * p

    return index


def spec(rows, last, phases, width=LANES):
    index = scan_map(phases)
    return pl.BlockSpec((rows, width), lambda p, j: (0, index(p, j, last)))


def fixed(*shape):
    return pl.BlockSpec(shape, lambda p, j: (0,) * len(shape))


def timetable(now, before, rate, slots, works):
    for stage, start in enumerate(slots):
        chunk, earlier = ((now - start) * rate) >> 4, ((before - start) * rate) >> 4
        base = 0
        for count, stages in works:
            local = chunk - base

            @pl.when((chunk != earlier) & (local >= 0) & (local < count))
            def _(stages=stages, local=local, stage=stage):
                stages[stage](local)

            base += count


def wind_up(now, rate, slots, works):
    steps = [(stages, k) for count, stages in works for k in range(count)]
    while any(((now - start) * rate) >> 4 < len(steps) - 1 for start in slots):
        now += 1
        for stage, start in enumerate(slots):
            k = ((now - start) * rate) >> 4
            if k != ((now - 1 - start) * rate) >> 4 and 0 <= k < len(steps):
                steps[k][0][stage](steps[k][1])
    for count, stages in works:
        lax.fori_loop(0, count, lambda k, _, s=stages[-1]: (s(k), 0)[1], 0)


def exchange(total_ref, sum_ref, totals_ref, sums_ref, send, recv):
    count = totals_ref.shape[0]
    me = lax.axis_index("seq")
    copies = []
    for o in range(1, count):
        peer = {"seq": lax.rem(me + o, count)}
        for i, (src, dst) in enumerate(((total_ref, totals_ref), (sum_ref, sums_ref))):
            copies.append(
                pltpu.make_async_remote_copy(
                    src_ref=src, dst_ref=dst.at[me], send_sem=send.at[i, o - 1],
                    recv_sem=recv.at[i, o - 1], device_id=peer, device_id_type=MESH,
                )
            )
    for copy in copies:
        copy.start()
    for copy in copies:
        copy.wait()


def forward_scan_kernel(
    tasks, numbers, depth, lead, nstate, pack_ref, act_ref, sel_ref, cut_ref, *refs
):
    hosted = len(tasks)
    srcs, refs = split_refs(refs, numbers)
    (step_ref, sig_ref, moment_ref, full_ref, keep_ref), refs = refs[:5], refs[5:]
    gouts, refs = refs[:hosted], refs[hosted:]
    (low, inb, outb, decay, drives, enter, befores, total_ref, sum_ref, totals_ref, sums_ref, send, recv), rest = refs[:13], refs[13:]
    count = act_ref.shape[0]
    rank = low.shape[1]
    wide = sel_ref.shape[1]
    p, j = pl.program_id(0), pl.program_id(1)
    blocks = pl.num_programs(1)
    turn = p * blocks + j
    me = lax.axis_index("seq")
    lanes = pl.ds(pl.multiple_of(j * LANES, LANES), LANES)
    gathers = [
        Gather(depth, layer, width, base, srcs[i], gouts[i], *rest[4 * i : 4 * i + 4])
        for i, (layer, width, base, _) in enumerate(tasks)
    ]

    @pl.when(turn == 0)
    def _():
        hail(depth)
        low[...] = sel_ref[:, :rank].astype(BF16)
        spread(inb, sel_ref, nstate, rank)
        spread(outb, sel_ref, nstate, rank + nstate)

    @pl.when(turn == 1)
    def _():
        await_hails(depth)
        for gather in gathers:
            lax.fori_loop(0, gather.count, lambda k, _, g=gather: (g.first(k), 0)[1], 0)

    works = [(gather.count, gather.stages()) for gather in gathers]
    pace, slots = 15, (2, 5, 9, 13)
    timetable(turn, turn - 1, pace, slots, works)

    @pl.when(p == 0)
    def _():
        stepw = pack_ref[0, wide : wide + rank, :]
        pre = jnp.dot(low[...], stepw, preferred_element_type=F32) + vector_of(pack_ref, 5)
        near = jnp.exp(-jnp.abs(pre))
        step_all = jnp.maximum(pre, 0.0) + jnp.log1p(near)
        step_ref[...] = step_all
        sig_ref[...] = jnp.where(pre >= 0.0, 1.0, near) / (1.0 + near)
        moment_ref[0:1, :] = jnp.sum(step_all, axis=0, keepdims=True)
        moment_ref[1:2, :] = jnp.sum(step_all * step_all, axis=0, keepdims=True)
        rate = rates_of(pack_ref, nstate)
        rates = rate_rows(rate, nstate)

        def body(pair, carry):
            states, sums = carry
            act = act_ref[pl.ds(pl.multiple_of(pair * 16, 16), 16), :].astype(F32)
            for half in (0, 1):
                at = pl.ds(pl.multiple_of(pair * 16 + half * 8, 8), 8)
                step = step_ref[at, :]
                away = step + cut_ref[at, :]
                drive = step * act[half * 8 : half * 8 + 8]
                drives[j, at, :] = drive
                sums = sums + away
                new = []
                for n in range(nstate):
                    gain = jnp.exp2(away * rates[n])
                    decay[j, n, at, :] = gain
                    new.append(gain * states[n] + drive * inb[n, at, :])
                states = tuple(new)
            return states, sums

        zero = jnp.zeros((CHUNKS, LANES), F32)
        ends, sums = lax.fori_loop(0, count // 16, body, ((zero,) * nstate, zero), unroll=2)
        entering, totals, before, total = chunk_links(ends, sums, rates, False)
        for n in range(nstate):
            enter[j, n] = entering[n]
        total_ref[:, lanes] = jnp.concatenate(totals, axis=0).astype(total_ref.dtype)
        befores[j] = before
        sum_ref[:, lanes] = total

    @pl.when(turn == blocks)
    def _():
        exchange(total_ref, sum_ref, totals_ref, sums_ref, send, recv)

    @pl.when(p == 1)
    def _():
        rate = rates_of(pack_ref, nstate)
        rates = rate_rows(rate, nstate)
        arrived = arriving_state(me, totals_ref, sums_ref, lanes, rate, False)
        before = befores[j]
        states = tuple(
            enter[j, n] + jnp.exp2(before * rates[n]) * arrived[n : n + 1, :] for n in range(nstate)
        )
        skip = jnp.broadcast_to(vector_of(pack_ref, 6), (CHUNKS, LANES))

        def body(pair, states):
            rows = pl.ds(pl.multiple_of(pair * 16, 16), 16)
            act = act_ref[rows, :].astype(F32)
            held = []
            for half in (0, 1):
                at = pl.ds(pl.multiple_of(pair * 16 + half * 8, 8), 8)
                held.append(states)
                drive = drives[j, at, :]
                out = skip * act[half * 8 : half * 8 + 8]
                new = []
                for n in range(nstate):
                    state = decay[j, n, at, :] * states[n] + drive * inb[n, at, :]
                    out = out + state * outb[n, at, :]
                    new.append(state)
                states = tuple(new)
                full_ref[at, :] = out
            for n in range(nstate):
                both = jnp.concatenate([held[0][n], held[1][n]], axis=0)
                keep_ref[0, n, rows, :] = both.astype(keep_ref.dtype)
            return states

        ends = lax.fori_loop(0, count // 16, body, states, unroll=2)
        for n in range(nstate):
            both = jnp.concatenate([ends[n], ends[n]], axis=0)
            keep_ref[0, n, count : count + 16, :] = both.astype(keep_ref.dtype)

    @pl.when(turn == 2 * lead - 1)
    def _():
        wind_up(2 * lead - 1, pace, slots, works)


def forward_scan(pack, nstate, act, selected, cut, sources, tasks, collective):
    count, inner = act.shape
    rank = selected.shape[1] - 2 * nstate
    depth = lax.axis_size("seq")
    blocks = inner // LANES
    last = blocks - 1
    arrays = [piece for source in sources for piece in pieces_of(source)]
    lengths = [sum(piece.shape[0] for piece in pieces_of(source)) for source in sources]
    anywhere = pl.BlockSpec(memory_space=pl.ANY)
    outs = pl.pallas_call(
        functools.partial(forward_scan_kernel, tasks, counts_of(sources), depth, blocks, nstate),
        grid=(2, blocks),
        in_specs=[
            pl.BlockSpec((1,) + pack.shape[1:], lambda p, j: (j, 0, 0)),
            spec(count, last, 2),
            fixed(*selected.shape),
            fixed(count, LANES),
        ]
        + [anywhere] * len(arrays),
        out_specs=[
            spec(count, last, 0),
            spec(count, last, 0),
            spec(2, last, 0),
            spec(count, last, 1),
            pl.BlockSpec((1, nstate, count + 16, LANES), lambda p, j: (j * p, 0, 0, 0)),
        ]
        + [anywhere] * len(tasks),
        out_shape=[
            jax.ShapeDtypeStruct((count, inner), F32),
            jax.ShapeDtypeStruct((count, inner), F32),
            jax.ShapeDtypeStruct((2, inner), F32),
            jax.ShapeDtypeStruct((count, inner), F32),
            jax.ShapeDtypeStruct((blocks, nstate, count + 16, LANES), BF16),
        ]
        + [gather_shape(r, t[3], depth, BF16) for r, t in zip(lengths, tasks)],
        scratch_shapes=[
            pltpu.VMEM((count, rank), BF16),
            pltpu.VMEM((nstate, count, LANES), F32),
            pltpu.VMEM((nstate, count, LANES), F32),
            pltpu.VMEM((blocks, nstate, count, LANES), F32),
            pltpu.VMEM((blocks, count, LANES), F32),
            pltpu.VMEM((blocks, nstate, CHUNKS, LANES), F32),
            pltpu.VMEM((blocks, CHUNKS, LANES), F32),
            pltpu.VMEM((nstate, inner), BF16),
            pltpu.VMEM((1, inner), F32),
            pltpu.VMEM((depth, nstate, inner), BF16),
            pltpu.VMEM((depth, 1, inner), F32),
            pltpu.SemaphoreType.DMA((2, depth - 1)),
            pltpu.SemaphoreType.DMA((2, depth - 1)),
        ]
        + gather_scratch([(r, t[3], t[1], BF16) for r, t in zip(lengths, tasks)], depth),
        compiler_params=pltpu.CompilerParams(
            dimension_semantics=("arbitrary", "arbitrary"), collective_id=collective,
            has_side_effects=True, vmem_limit_bytes=VMEM_LIMIT,
        ),
        name="forward_scan",
    )(pack, act, selected, cut, *arrays)
    return outs[:5], [flat_rows(out) for out in outs[5:]]


def backward_scan_kernel(
    tasks, numbers, homes, olds, depth, lead, nstate, dfull_ref, step_ref, cut_ref, pack_ref, sel_ref, act_ref, sig_ref,
    keep_ref, *refs
):
    srcs, refs = split_refs(refs, numbers)
    refs = refs[olds:]
    (dact_ref, gbias_ref, gskip_ref, gdecay_ref, gstepw_ref, dsel_ref), refs = refs[:6], refs[6:]
    gouts, refs = refs[:homes], refs[homes:]
    (
        low, inb, outb, decay, enter, befores, total_ref, sum_ref, totals_ref, sums_ref,
        din_acc, dout_acc, decay_acc, dlow_acc, dstep_buf, send, recv,
    ), rest = refs[:17], refs[17:]
    count = act_ref.shape[0]
    rank = low.shape[1]
    wide = sel_ref.shape[1]
    pairs = count // 16
    p, j = pl.program_id(0), pl.program_id(1)
    blocks = pl.num_programs(1)
    turn = p * blocks + j
    me = lax.axis_index("seq")
    lanes = pl.ds(pl.multiple_of(j * LANES, LANES), LANES)
    items = [
        Reduce(depth, layer, width, base, srcs[i], gouts[home], *rest[9 * i : 9 * i + 9])
        for i, (layer, width, home, base) in enumerate(tasks)
    ]

    @pl.when(turn == 0)
    def _():
        hail(depth)
        low[...] = sel_ref[:, :rank].astype(BF16)
        spread(inb, sel_ref, nstate, rank)
        spread(outb, sel_ref, nstate, rank + nstate)
        din_acc[...] = jnp.zeros_like(din_acc)
        dout_acc[...] = jnp.zeros_like(dout_acc)
        dlow_acc[...] = jnp.zeros_like(dlow_acc)

    @pl.when(turn == 1)
    def _():
        await_hails(depth)

    works = [(item.count, item.stages()) for item in items]
    pace, slots = 6 if len(works) > 2 else 4, (2, 4, 9, 14, 18)
    timetable(turn + p * j, turn - 1 + p * jnp.maximum(j - 1, 0), pace, slots, works)

    @pl.when(p == 0)
    def _():
        rate = rates_of(pack_ref, nstate)
        rates = rate_rows(rate, nstate)

        def body(step_back, carry):
            states, sums = carry
            pair = pairs - 1 - step_back
            for half in (1, 0):
                at = pl.ds(pl.multiple_of(pair * 16 + half * 8, 8), 8)
                away = step_ref[at, :] + cut_ref[at, :]
                grad = dfull_ref[at, :]
                sums = sums + away
                new = []
                for n in range(nstate):
                    gain = jnp.exp2(away * rates[n])
                    decay[j, n, at, :] = gain
                    new.append(gain * (states[n] + outb[n, at, :] * grad))
                states = tuple(new)
            return states, sums

        zero = jnp.zeros((CHUNKS, LANES), F32)
        ends, sums = lax.fori_loop(0, pairs, body, ((zero,) * nstate, zero), unroll=2)
        entering, totals, before, total = chunk_links(ends, sums, rates, True)
        for n in range(nstate):
            enter[j, n] = entering[n]
        total_ref[:, lanes] = jnp.concatenate(totals, axis=0).astype(total_ref.dtype)
        befores[j] = before
        sum_ref[:, lanes] = total

    @pl.when(turn == blocks)
    def _():
        exchange(total_ref, sum_ref, totals_ref, sums_ref, send, recv)

    @pl.when(p == 1)
    def _():
        rate = rates_of(pack_ref, nstate)
        rates = rate_rows(rate, nstate)
        arrived = arriving_state(me, totals_ref, sums_ref, lanes, rate, True)
        before = befores[j]
        states = tuple(
            enter[j, n] + jnp.exp2(before * rates[n]) * arrived[n : n + 1, :] for n in range(nstate)
        )
        skip = jnp.broadcast_to(vector_of(pack_ref, 6), (CHUNKS, LANES))
        for n in range(nstate):
            decay_acc[n] = jnp.zeros((CHUNKS, LANES), F32)
            last = keep_ref[0, n, count : count + 16, :].astype(F32)[0:CHUNKS]
            dout_acc[n, pl.ds(count, CHUNKS), :] += last * dfull_ref[pl.ds(count - CHUNKS, CHUNKS), :]

        def body(step_back, carry):
            states, gskip = carry
            pair = pairs - 1 - step_back
            rows = pl.ds(pl.multiple_of(pair * 16, 16), 16)
            act = act_ref[rows, :].astype(F32)
            held = [keep_ref[0, n, rows, :].astype(F32) for n in range(nstate)]
            sums = [None] * nstate
            for half in (1, 0):
                at = pl.ds(pl.multiple_of(pair * 16 + half * 8, 8), 8)
                step = step_ref[at, :]
                act_now = act[half * 8 : half * 8 + 8]
                drive = step * act_now
                grad = dfull_ref[at, :]
                gskip = gskip + grad * act_now
                if half:
                    earlier = dfull_ref[pl.ds(pl.multiple_of(pair * 16, 8), 8), :]
                else:
                    earlier = dfull_ref[pl.ds(pl.multiple_of(jnp.maximum(pair * 16 - 8, 0), 8), 8), :]
                by_rate = jnp.zeros((CHUNKS, LANES), F32)
                mapped = jnp.zeros((CHUNKS, LANES), F32)
                new = []
                for n in range(nstate):
                    prior = held[n][half * 8 : half * 8 + 8]
                    adjoint = states[n] + outb[n, at, :] * grad
                    passed = adjoint * decay[j, n, at, :]
                    rho = passed * prior
                    by_rate = by_rate + rho * rates[n]
                    mapped = mapped + adjoint * inb[n, at, :]
                    sums[n] = rho * step if half else sums[n] + rho * step
                    din_acc[n, at, :] += adjoint * drive
                    dout_acc[n, at, :] += prior * earlier
                    new.append(passed)
                states = tuple(new)
                dstep_buf[at, :] = by_rate * LN2 + act_now * mapped
                dact_ref[at, :] = step * mapped + skip * grad
            for n in range(nstate):
                decay_acc[n] += sums[n]
            return states, gskip

        _, gskip = lax.fori_loop(0, pairs, body, (states, jnp.zeros((CHUNKS, LANES), F32)), unroll=2)
        gskip_ref[...] = jnp.sum(gskip, axis=0, keepdims=True)
        decays = [jnp.sum(decay_acc[n], axis=0, keepdims=True) for n in range(nstate)]
        gdecay = (rate * LN2) * jnp.concatenate(decays, axis=0)
        gdecay_ref[0] = gdecay.astype(gdecay_ref.dtype)
        dpre = dstep_buf[...] * sig_ref[...]
        gbias_ref[...] = jnp.sum(dpre, axis=0, keepdims=True)
        low_dpre = dpre.astype(BF16)
        gstepw_ref[0] = lax.dot_general(
            low[...], low_dpre, (((0,), (0,)), ((), ())), preferred_element_type=F32
        ).astype(gstepw_ref.dtype)
        dlow_acc[...] += lax.dot_general(
            low_dpre, pack_ref[0, wide : wide + rank, :], (((1,), (1,)), ((), ())),
            preferred_element_type=F32,
        )

    @pl.when(turn == 2 * lead - 1)
    def _():
        column = lax.broadcasted_iota(jnp.int32, (LANES, nstate), 1)
        din = jnp.zeros((count, nstate), F32)
        dout = jnp.zeros((count, nstate), F32)
        for n in range(nstate):
            pick = (column == n).astype(BF16)
            din = din + jnp.dot(din_acc[n].astype(BF16), pick, preferred_element_type=F32)
            part = dout_acc[n, CHUNKS : count + CHUNKS, :].astype(BF16)
            dout = dout + jnp.dot(part, pick, preferred_element_type=F32)
        dsel_ref[...] = jnp.concatenate([dlow_acc[...], din, dout], axis=1).astype(BF16)

    @pl.when(turn == 2 * lead - 1)
    def _():
        wind_up(3 * lead - 2, pace, slots, works)


def backward_scan(
    dfull, step, cut, pack, nstate, selected, act, sig, keep, sources, tasks, homes, collective
):
    count, inner = act.shape
    rank = selected.shape[1] - 2 * nstate
    depth = lax.axis_size("seq")
    blocks = inner // LANES
    last = blocks - 1
    arrays = [by_chip(piece, depth) for source in sources for piece in pieces_of(source)]
    olds = {i: home for i, home in enumerate(homes) if not isinstance(home, tuple)}
    shapes = [home if isinstance(home, tuple) else home.shape for home in homes]
    anywhere = pl.BlockSpec(memory_space=pl.ANY)
    outs = pl.pallas_call(
        functools.partial(
            backward_scan_kernel, tasks, counts_of(sources), len(homes), len(olds), depth, blocks, nstate
        ),
        grid=(2, blocks),
        in_specs=[
            spec(count, last, 2),
            spec(count, last, 2),
            fixed(count, LANES),
            pl.BlockSpec((1,) + pack.shape[1:], lambda p, j: (j, 0, 0)),
            fixed(*selected.shape),
            spec(count, last, 1),
            spec(count, last, 1),
            pl.BlockSpec((1, nstate, count + 16, LANES), lambda p, j: (j * p, 0, 0, 0)),
        ]
        + [anywhere] * (len(arrays) + len(olds)),
        out_specs=[
            spec(count, last, 1),
            spec(1, last, 1),
            spec(1, last, 1),
            pl.BlockSpec((1, nstate, LANES), lambda p, j: (j * p, 0, 0)),
            pl.BlockSpec((1, rank, LANES), lambda p, j: (j * p, 0, 0)),
            fixed(*selected.shape),
        ]
        + [anywhere] * len(homes),
        out_shape=[
            jax.ShapeDtypeStruct((count, inner), F32),
            jax.ShapeDtypeStruct((1, inner), F32),
            jax.ShapeDtypeStruct((1, inner), F32),
            jax.ShapeDtypeStruct((blocks, nstate, LANES), BF16),
            jax.ShapeDtypeStruct((blocks, rank, LANES), BF16),
            jax.ShapeDtypeStruct(selected.shape, BF16),
        ]
        + [jax.ShapeDtypeStruct(shape, F32) for shape in shapes],
        scratch_shapes=[
            pltpu.VMEM((count, rank), BF16),
            pltpu.VMEM((nstate, count, LANES), F32),
            pltpu.VMEM((nstate, count, LANES), F32),
            pltpu.VMEM((blocks, nstate, count, LANES), F32),
            pltpu.VMEM((blocks, nstate, CHUNKS, LANES), F32),
            pltpu.VMEM((blocks, CHUNKS, LANES), F32),
            pltpu.VMEM((nstate, inner), BF16),
            pltpu.VMEM((1, inner), F32),
            pltpu.VMEM((depth, nstate, inner), BF16),
            pltpu.VMEM((depth, 1, inner), F32),
            pltpu.VMEM((nstate, count, LANES), F32),
            pltpu.VMEM((nstate, count + CHUNKS, LANES), F32),
            pltpu.VMEM((nstate, CHUNKS, LANES), F32),
            pltpu.VMEM((count, rank), F32),
            pltpu.VMEM((count, LANES), F32),
            pltpu.SemaphoreType.DMA((2, depth - 1)),
            pltpu.SemaphoreType.DMA((2, depth - 1)),
        ]
        + reduce_scratch([shard_of(s) + (t[1], BF16) for s, t in zip(sources, tasks)], depth),
        input_output_aliases={8 + len(arrays) + n: 6 + i for n, i in enumerate(olds)},
        compiler_params=pltpu.CompilerParams(
            dimension_semantics=("arbitrary", "arbitrary"), collective_id=collective,
            has_side_effects=True, vmem_limit_bytes=VMEM_LIMIT,
        ),
        name="backward_scan",
    )(dfull, step, cut, pack, selected, act, sig, keep, *arrays, *olds.values())
    return outs[:6], outs[6:]


def places(lengths, count, reach):
    steps = count // CHUNKS
    base = lax.axis_index("seq") * count
    starts = jnp.cumsum(lengths) - lengths
    here = (
        base + jnp.arange(steps, dtype=jnp.int32)[:, None]
        + steps * jnp.arange(CHUNKS, dtype=jnp.int32)[None, :]
    )

    def segment(at):
        return jnp.sum((starts[:, None, None] <= at[None]).astype(jnp.int32), axis=0) - 1

    own = segment(here)
    same = jnp.stack(
        [(segment(here - reach + k) == own).astype(F32).reshape(count) for k in range(reach)]
    )
    same = jnp.broadcast_to(same[:, :, None], same.shape + (LANES,))
    opens = jnp.any(starts[:, None, None] == here[None], axis=0)
    cut = jnp.where(opens, CUT, 0.0).astype(F32).reshape(count, 1)
    return same, jnp.broadcast_to(cut, (count, LANES))


def layer_forward(xin, in_conv, other, same, cut, host, collective):
    pack, gain, wide, nstate = other
    count = xin.shape[0]
    inner = in_conv.shape[1]
    reach = same.shape[0]
    scale = lax.rsqrt(jnp.mean(xin * xin, axis=-1, keepdims=True) + EPS)
    normed = (xin * scale * gain).astype(BF16)
    conv_in = jnp.dot(normed, in_conv, preferred_element_type=F32).astype(BF16)
    last = conv_in[(count - reach * CHUNKS) :].reshape(reach, CHUNKS, inner)[:, CHUNKS - 1]
    halo = shifted(last, "seq", 1)
    act, selected = select_call(conv_in, halo, same, pack, wide)
    (step, sig, moments, full, keep), got = forward_scan(
        pack, nstate, act, selected, cut, host[0], host[1], collective
    )
    return (scale, normed, conv_in, halo, act, selected, step, sig, full, keep), moments, got


def layer_output(xin, normed, full, in_gate, out_weight):
    gate = jnp.dot(normed, in_gate, preferred_element_type=F32).astype(BF16)
    wide = gate.astype(F32)
    gated = (full * (wide * jax.nn.sigmoid(wide))).astype(BF16)
    return xin + jnp.dot(gated, out_weight, preferred_element_type=F32), gate, gated


def outer_sum(left, right):
    return lax.dot_general(left, right, (((0,), (0,)), ((), ())), preferred_element_type=F32)


def times_transposed(left, right):
    return lax.dot_general(left, right, (((1,), (1,)), ((), ())), preferred_element_type=F32)


def layer_backward(grad_out, weights, same, cut, saved, moments, host, collective):
    in_conv, in_gate, out_weight, pack, gain, _, nstate = weights
    (xin, scale, normed, conv_in, halo, act, selected, step, sig, full, keep, gate, gated) = saved
    count, inner = act.shape
    reach = same.shape[0]
    grad_low = grad_out.astype(BF16)
    dgated = times_transposed(grad_low, out_weight)
    gout = outer_sum(gated, grad_low).astype(BF16)
    wide = gate.astype(F32)
    dfull = dgated * (wide * jax.nn.sigmoid(wide))
    dgate = (dgated * full * silu_slope(wide)).astype(BF16)
    gin_gate = outer_sum(normed, dgate).astype(BF16)
    sources, tasks, homes = host(gout, gin_gate)
    (dact, gbias, gskip, gdecay, gstepw, dsel), found = backward_scan(
        dfull, step, cut, pack, nstate, selected, act, sig, keep, sources, tasks, homes, collective
    )
    dconv, tail, spill, gsel, gsmall = conv_grad(
        conv_in, halo, same, pack, act, dact, dsel, gbias, gskip
    )
    late = (tail + shifted(spill, "seq", -1)).astype(BF16)
    grid = dconv.reshape(count // CHUNKS, CHUNKS, inner)
    dconv = grid.at[count // CHUNKS - reach :, CHUNKS - 1].set(late).reshape(count, inner)
    gin_conv = outer_sum(normed, dconv).astype(BF16)
    dnormed = times_transposed(dconv, in_conv) + times_transposed(dgate, in_gate)
    unit = xin * scale
    ggain = jnp.sum(dnormed * unit, axis=0)
    dunit = dnormed * gain
    grad_in = scale * (dunit - unit * jnp.mean(dunit * unit, axis=-1, keepdims=True)) + grad_out
    shards = lax.axis_size(("dp", "seq"))
    per = inner // shards
    if per < LANES:
        blocked = lambda rows: rows.swapaxes(0, 1).reshape(rows.shape[1], shards, per).swapaxes(0, 1)
        gsel, gstepw, gdecay, gsmall = (blocked(rows) for rows in (gsel, gstepw, gdecay, gsmall))
    ggain = jnp.pad(ggain.reshape(shards, 1, -1), ((0, 0), (0, 0), (0, per - ggain.shape[0] // shards)))
    moments = moments.reshape(2, shards, per).swapaxes(0, 1)
    rest = jnp.concatenate([ggain, moments, jnp.zeros((shards, 5, per), F32)], axis=1)
    rest = jnp.concatenate([gsmall, rest], axis=1).astype(BF16)
    rows = ([gsel], [gstepw, gdecay, rest])
    return grad_in, gin_conv, gin_gate, gout, rows, found


AXES = ("section", "dp", "seq")


def body(
    inputs, doc_lengths, out_grad, norm_gain, in_weight, conv_weight, conv_bias, select_weight,
    step_weight, step_bias, log_decay, skip_gain, out_weight,
):
    section = lax.axis_index("section")
    micro, _, count, model = inputs.shape
    taps, per = conv_weight.shape[1:]
    shards = lax.axis_size(("dp", "seq"))
    inner = per * shards
    rank, nstate = step_weight.shape[1], log_decay.shape[1]
    wide = rank + 2 * nstate

    kernels = lax.axis_size("dp") == 4 and per % LANES == 0 and in_weight.shape[1] % 32 == 0
    pad = per - norm_gain.shape[1]
    vectors = [conv_weight[0], conv_bias, step_bias, skip_gain, jnp.pad(norm_gain, ((0, 0), (0, pad)))]
    vectors = [v.astype(F32) for v in vectors] + [jnp.zeros((16 - taps - 4, per), F32)]
    vectors = jnp.concatenate(vectors, axis=0).astype(BF16)
    pieces = [select_weight[0].T, step_weight[0], log_decay[0], vectors]
    in_half, out_half = in_weight[0], out_weight[0]
    if kernels:
        length = sum(piece.shape[0] for piece in pieces)
        quarter = in_half.shape[:1] + (inner,)
        packs = gather_rows(
            pieces + [in_half], [((0,), (1, 2, 3)), 4, 4],
            [(0, per, 0), (0, 256, 0), (0, 256, inner)],
            [(length, per), quarter, quarter], None, 2,
        )
        packed = [packs[0].reshape(shards, -1, per), None]
        in_conv, in_gate = [packs[1], None], [packs[2], None]
        outs_weight = [None, None]
        hosts = [
            (
                [([pieces[0]], pieces[1:]), in_half, out_half],
                [(1, per, 0, per), (1, 256, 0, inner), (0, 128, 0, model)],
            ),
            ([in_half, out_half], [(1, 256, inner, inner), (1, 128, 0, model)]),
        ]
    else:
        packed = lax.all_gather(jnp.concatenate(pieces, axis=0), AXES, axis=0).reshape(2, shards, -1, per)
        in_all = lax.all_gather(in_half, AXES, axis=0, tiled=True).reshape(2, model, -1)
        in_conv, in_gate = in_all[:, :, :inner], in_all[:, :, inner:]
        outs_weight = lax.all_gather(out_half, AXES, axis=0, tiled=True).reshape(2, inner, model)
        hosts = [([], []), ([], [])]
    def other(layer):
        pack = packed[layer]
        gain = pack[:, wide + rank + nstate + taps + 3, : norm_gain.shape[1]].reshape(-1).astype(F32)
        if per < LANES:
            flat = pack.swapaxes(0, 1).reshape(-1, inner)
            pack = flat.reshape(-1, inner // LANES, LANES).swapaxes(0, 1)
        return pack, gain, wide, nstate

    mine = lambda value: lax.dynamic_index_in_dim(value, section, 0, keepdims=False)[0]
    same, cut = places(mine(doc_lengths), count, taps - 1)
    state = interleave(mine(inputs).astype(F32))
    outs, kept, weights = [], [], []
    for layer in range(2):
        saved, moments, got = layer_forward(
            state, in_conv[layer], other(layer), same, cut, hosts[layer], 5 + layer
        )
        if kernels:
            if layer == 0:
                packed[1] = got.pop(0).reshape(shards, -1, per)
            (in_gate if layer else in_conv)[1], outs_weight[layer] = got
        result, gate, gated = layer_output(
            state, saved[1], saved[8], in_gate[layer], outs_weight[layer]
        )
        weights.append((in_conv[layer], in_gate[layer], outs_weight[layer]) + other(layer))
        kept.append(((state,) + saved + (gate, gated), moments))
        state = result
        outs.append(state)
    grad = interleave(mine(out_grad).astype(F32))
    def split(value):
        return value.reshape(shards, -1, value.shape[1])

    grads = [None] * 2
    parts = [None] * 2
    found = []
    for layer in (1, 0):
        if not kernels:
            host = lambda gout, gin_gate: ([], [], [])
        elif layer == 1:
            host = lambda gout, gin_gate: (
                [split(gout), split(gin_gate)], [(1, 256, 0, 0), (1, 512, 1, inner)],
                [(per, model), (in_half.shape[0], 2 * inner)],
            )
        else:
            host = lambda gout, gin_gate: (
                [split(gout), parts[1][1], parts[1][0], split(gin_gate)],
                [(0, 256, 0, 0), (1, 512, 1, 0), (1, per, 2, 0), (0, 512, 1, inner)],
                list(found) + [(length, per)],
            )
        grad, gin_conv, gin_gate, gout, pack, found = layer_backward(
            grad, weights[layer], same, cut, *kept[layer], host, 7 + layer
        )
        grads[layer] = grad
        parts[layer] = [pack, split(gin_conv), split(gin_gate), split(gout)]

    if kernels:
        results, (gin, rows) = reduce_rows(
            [parts[0][1], parts[0][0]], [(0, 256, 0, 0), (0, per, 1, 0)], [found[1], (length, per)],
            outs + grads, 3,
        )
        rows = jnp.where(section == 0, rows, found[2])
        gout = found[0]
    else:
        found = []
        for side in parts:
            side[0] = jnp.concatenate(pieces_of(side[0]), axis=1)
        for pair in zip(*parts):
            both = jnp.stack(pair).reshape((-1,) + pair[0].shape[1:])
            found.append(lax.psum_scatter(both, AXES, scatter_dimension=0).astype(F32))
        rows, gin_conv, gin_gate, gout = found
        gin = jnp.concatenate([gin_conv, gin_gate], axis=1)

    def place(values):
        first, second = (in_order(value) for value in values)
        own = jnp.where(section == 0, first, second)
        other = jnp.where(section == 0, second, first)
        other = lax.ppermute(other, "section", [(0, 1), (1, 0)])
        both = jnp.stack([jnp.where(section == 0, own, other), jnp.where(section == 0, other, own)])
        return both

    both = (1, micro, 1, count, model)
    at = wide + rank + nstate
    tokens = micro * inputs.shape[1] * lax.axis_size("dp") * count * lax.axis_size("seq")
    if not kernels:
        results = place(outs), place(grads)
    return (
        results[0].reshape(both),
        results[1].reshape(both),
        rows[at + 8, : norm_gain.shape[1]][None],
        gin[None],
        rows[at : at + taps][None],
        rows[at + taps][None],
        rows[:wide].T[None],
        rows[wide : wide + rank][None],
        rows[at + taps + 1][None],
        rows[wide + rank : at][None],
        rows[at + taps + 2][None],
        gout[None],
        (rows[at + 9 : at + 11] / tokens)[None],
    )


def solution(mesh):
    vector = P("section", ("dp", "seq"))
    matrix = P("section", ("dp", "seq"), None)
    turned = P("section", None, ("dp", "seq"))
    tokens = P(None, "dp", "seq", None)
    in_specs = (
        tokens, P(None, "dp", None), tokens, vector, matrix, turned, vector, matrix, turned,
        vector, turned, vector, matrix,
    )
    result = P("section", None, "dp", "seq", None)
    out_specs = (
        result, result, vector, matrix, turned, vector, matrix, turned, vector, turned, vector,
        matrix, turned,
    )
    return jax.shard_map(body, mesh=mesh, in_specs=in_specs, out_specs=out_specs, check_vma=False)
```

profile of v0, /device:TPU:0, one launch (start us, length us, event | category | flops | bytes accessed | tf_op | source)
XLA Modules:
  0.0 500.0 jit_solution(8413875275626626173)
XLA Ops:
  0.7 2.1 constant_dynamic-slice_fusion
  3.1 1.2 concatenate.33.refs_3_
  4.2 56.0 %gather_rows.1 = (bf16[2,2,4,2,96,128]{5,4,3,2,1,0:T(8,128)(2,1)}, bf16[2,2,4,2,32,2048]{5,4,3,2,1,0:T(8,128)(2,1)}, bf16[2,2,4,2,32,2048]{5,4,3,2,1,0:T(8,128)(2,1)}) custom-call(bf16[96,128]{1,0:T(8,128)(2,1)} %bitcast.189, bf16[64,128]{1,0:T(8,128)(2,1)} %bitcast.193, bf16[16,128]{1,0:T(8,128)(2,1)} %bitcast.197, bf16[16,128]{1,0:T(8,128)(2,1)} %concatenate.33.refs_3_, ...), custom_call_target="tpu_custom_call" | custom-call | tf_op jit(solution)/shard_map/gather_rows/pallas_call | solution.py:487
  61.3 3.7 convolution_convert_fusion.8.conv_ref
  65.0 1.0 copy-done.7
  66.1 3.3 collective-permute-start
  69.4 1.1 convert_bitcast_fusion
  71.6 4.5 convolution_convert_fusion.7
  76.3 1.0 broadcast_in_dim.29.same_ref
  77.3 4.5 conv_select.2
  82.5 60.3 %forward_scan.2 = (f32[256,2048]{1,0:T(8,128)}, f32[256,2048]{1,0:T(8,128)}, f32[2,2048]{1,0:T(2,128)}, f32[256,2048]{1,0:T(8,128)}, bf16[16,16,272,128]{3,2,1,0...) custom-call(bf16[16,192,128]{2,1,0:T(8,128)(2,1)} %bitcast.154, ...), custom_call_target="tpu_custom_call" | custom-call | tf_op jit(solution)/shard_map/forward_scan/pallas_call | solution.py:1011
  143.7 5.4 %multiply_reduce_fusion.4 = (f32[256]{0:T(256)S(1)}, f32[256,1024]{1,0:T(8,128)S(1)}) fusion(bf16[2048,1024]{1,0:T(8,128)(2,1)} %bitcast.210, f32[256,2048]{1,0:T(8,128)} %get-tuple-element.94, bf16[256,2048]{1,0:T(8,128)(2,1)} %convolution_convert_fusion.7, f32[32,8,1024]{2,0,1:T(8,128)} %convert_bitcast_fusion), kind=kOutput, calls=%fused_computation.52 | convolution fusion | flops 1078198016 | bytes 9438208 | tf_op jit(solution)/shard_map/dot_general | solution.py:1346
  149.3 1.3 convolution_convert_fusion.6.conv_ref
  150.6 1.0 copy-done.8
  151.6 4.6 collective-permute-start.1
  156.2 0.9 collective-permute-done.1.halo_ref
  157.7 4.5 conv_select.3
  162.2 57.7 %forward_scan.3 = (f32[256,2048]{1,0:T(8,128)}, f32[256,2048]{1,0:T(8,128)}, f32[2,2048]{1,0:T(2,128)}, f32[256,2048]{1,0:T(8,128)}, bf16[16,16,272,128]{3,2,1,0...) custom-call(bf16[16,192,128]{2,1,0:T(8,128)(2,1)} %bitcast.159, ...), custom_call_target="tpu_custom_call" | custom-call | tf_op jit(solution)/shard_map/forward_scan/pallas_call | solution.py:1011
  220.0 3.9 fusion.23
  224.2 3.4 fusion.13
  227.6 3.8 convolution_convert_fusion.4
  231.4 3.3 convolution_convert_fusion.3
  234.7 69.5 %backward_scan.2 = (f32[256,2048]{1,0:T(8,128)}, f32[1,2048]{1,0:T(1,128)}, f32[1,2048]{1,0:T(1,128)}, bf16[16,16,128]{2,1,0:T(8,128)(2,1)}, bf16[16,64,128]{2,1...) custom-call(f32[256,2048]{1,0:T(8,128)} %get-tuple-element.219.dfull_ref, ...), custom_call_target="tpu_custom_call" | custom-call | tf_op jit(solution)/shard_map/backward_scan/pallas_call | solution.py:1239
  304.3 6.4 %conv_grad.2 = (bf16[256,2048]{1,0:T(8,128)(2,1)}, f32[3,2048]{1,0:T(4,128)}, f32[3,2048]{1,0:T(4,128)}, bf16[16,96,128]{2,1,0:T(8,128)(2,1)}, f32[16,8,128]{2,1,0:T(8,128)}) custom-call(bf16[256,2048]{1,0:T(8,128)(2,1)} %copy-done.8, bf16[3,2048]{1,0:T(4,128)(2,1)} %copy-done.24, f32[3,256,128]{2,1,0:T(8,128)} %broadcast_in_dim.29.same_ref, ...), custom_call_target="tpu_custom_call" | custom-call | tf_op jit(solution)/shard_map/conv_grad/pallas_call | solution.py:241
  310.7 1.3 collective-permute-start.2
  312.3 0.8 convert.57
  313.1 3.6 collective-permute-done.2
  317.5 1.6 scatter.6
  319.1 3.9 fusion.17
  323.4 1.5 multiply_reduce_fusion.2
  325.8 1.0 copy-done.38
  327.0 3.3 fusion.6
  330.3 3.5 convolution_convert_fusion.2
  333.8 3.3 convolution_convert_fusion.1
  337.3 3.8 convolution_convert_fusion
  341.8 79.7 %backward_scan.3 = (f32[256,2048]{1,0:T(8,128)}, f32[1,2048]{1,0:T(1,128)}, f32[1,2048]{1,0:T(1,128)}, bf16[16,16,128]{2,1,0:T(8,128)(2,1)}, bf16[16,64,128]{2,1...) custom-call(f32[256,2048]{1,0:T(8,128)} %get-tuple-element.217.dfull, ...), custom_call_target="tpu_custom_call", output_to_operand_aliasing={{6}: (15, {}), {7}: (16, {})} | custom-call | tf_op jit(solution)/shard_map/backward_scan/pallas_call | solution.py:1239
  421.6 6.3 %conv_grad.3 = (bf16[256,2048]{1,0:T(8,128)(2,1)}, f32[3,2048]{1,0:T(4,128)}, f32[3,2048]{1,0:T(4,128)}, bf16[16,96,128]{2,1,0:T(8,128)(2,1)}, f32[16,8,128]{2,1,0:T(8,128)}) custom-call(bf16[256,2048]{1,0:T(8,128)(2,1)} %copy-done.7, bf16[3,2048]{1,0:T(4,128)(2,1)} %copy-done.23, f32[3,256,128]{2,1,0:T(8,128)} %broadcast_in_dim.29.same_ref, ...), custom_call_target="tpu_custom_call" | custom-call | tf_op jit(solution)/shard_map/conv_grad/pallas_call | solution.py:241
  427.9 1.4 collective-permute-start.3
  429.4 5.7 %convolution_add_fusion.2.refs_1_ = f32[256,1024]{1,0:T(8,128)} fusion(f32[256,1024]{1,0:T(8,128)} %copy-done, bf16[2048,1024]{1,0:T(8,128)(2,1)} %bitcast.209, f32[256,2048]{1,0:T(8,128)} %get-tuple-element.101, bf16[256,2048]{1,0:T(8,128)(2,1)} %copy-done.42), kind=kOutput, calls=%fused_computation.34 | convolution fusion | flops 1077673984 | bytes 9437184 | tf_op jit(solution)/shard_map/dot_general | solution.py:1346
  435.6 3.5 fusion.14
  439.2 3.4 bitcast_convert_fusion
  442.8 1.9 multiply_reduce_fusion
  444.8 1.6 multiply_add_fusion.refs_2_
  447.2 40.1 %reduce_rows.1 = (f32[2,256,1024]{2,1,0:T(8,128)}, f32[2,256,1024]{2,1,0:T(8,128)}, f32[64,4096]{1,0:T(8,128)}, f32[192,128]{1,0:T(8,128)}) custom-call(f32[256,1024]{1,0:T(8,128)} %copy-done, f32[256,1024]{1,0:T(8,128)} %convolution_add_fusion.2.refs_1_, f32[256,1024]{1,0:T(8,128)} %multiply_add_fusion.refs_2_, ...), custom_call_target="tpu_custom_call", output_to_operand_aliasing={{2}: (9, {})} | custom-call | tf_op jit(solution)/shard_map/reduce_rows/pallas_call | solution.py:789
  487.3 0.9 broadcast_select_fusion
  492.2 3.3 copy.143
  495.5 1.3 copy.144
  497.5 1.0 copy.145
  (153 shorter events, 16.1 us)
Async XLA Ops:
  0.6 2.3 copy-start.40
  0.7 2.4 copy-start.32
  0.7 2.4 copy-start.31
  0.7 2.4 copy-start.30
  0.7 2.4 copy-start.29
  61.3 10.3 %copy-start.20 = (bf16[32,8,1024]{2,0,1:T(8,128)(2,1)}, bf16[32,8,1024]{2,0,1:T(8,128)(2,1)S(1)}, u32[]{:S(2)}) copy-start(bf16[32,8,1024]{2,0,1:T(8,128)(2,1)S(1)} %multiply_convert_fusion.4) | copy-start | bytes 1572868
  61.3 9.3 %copy-start.33 = (s32[2,1,4]{2,1,0:T(1,128)S(1)}, s32[2,1,4]{2,1,0:T(1,128)}, u32[]{:S(2)}) copy-start(s32[2,1,4]{2,1,0:T(1,128)} %param.18) | copy-start | bytes 100
  65.0 1.0 copy-start.7
  66.1 10.2 %collective-permute-start = (bf16[3,2048]{1,0:T(4,128)(2,1)S(1)}, bf16[3,2048]{1,0:T(4,128)(2,1)S(1)}, u32[]{:S(2)}, u32[]{:S(2)}) collective-permute-start(bf16[3,2048]{1,0:T(4,128)(2,1)S(1)} %bitcast.201), channel_id=1, source_target_pairs={{0,1},{1,2},{2,3},{4,5},{5,6},{6,7},{8,9},{9,10},{10,11},{12,13},{... | collective-permute-start | bytes 36872 | tf_op jit(solution)/shard_map/ppermute | solution.py:277
  76.3 1.0 copy-start.23
  143.7 5.6 %copy-start.36 = (bf16[2,2,4,2,32,2048]{5,4,3,2,1,0:T(8,128)(2,1)S(1)}, bf16[2,2,4,2,32,2048]{5,4,3,2,1,0:T(8,128)(2,1)}, u32[]{:S(2)}) copy-start(bf16[2,2,4,2,32,2048]{5,4,3,2,1,0:T(8,128)(2,1)} %get-tuple-element.98) | copy-start | bytes 12582916
  149.1 1.5 copy-start
  150.6 1.0 copy-start.8
  151.6 5.5 %collective-permute-start.1 = (bf16[3,2048]{1,0:T(4,128)(2,1)S(1)}, bf16[3,2048]{1,0:T(4,128)(2,1)S(1)}, u32[]{:S(2)}, u32[]{:S(2)}) collective-permute-start(bf16[3,2048]{1,0:T(4,128)(2,1)S(1)} %bitcast.202), channel_id=1, source_target_pairs={{0,1},{1,2},{2,3},{4,5},{5,6},{6,7},{8,9},{9,10},{10,11},{12,13},{... | collective-permute-start | bytes 36872 | tf_op jit(solution)/shard_map/ppermute | solution.py:277
  157.1 0.6 copy-start.24
  220.0 3.9 copy-start.9
  220.0 4.3 copy-start.37
  224.2 3.4 copy-start.15
  227.6 3.8 copy-start.42
  227.6 3.8 copy-start.11
  304.2 8.0 %copy-start.27 = (f32[2,2048]{1,0:T(2,128)S(1)}, f32[2,2048]{1,0:T(2,128)}, u32[]{:S(2)}) copy-start(f32[2,2048]{1,0:T(2,128)} %get-tuple-element.135) | copy-start | bytes 49156
  304.3 8.0 %copy-start.28 = (f32[2,2048]{1,0:T(2,128)S(1)}, f32[2,2048]{1,0:T(2,128)}, u32[]{:S(2)}) copy-start(f32[2,2048]{1,0:T(2,128)} %get-tuple-element.121) | copy-start | bytes 49156
  310.7 6.0 %collective-permute-start.2 = (f32[3,2048]{1,0:T(4,128)}, f32[3,2048]{1,0:T(4,128)S(1)}, u32[]{:S(2)}, u32[]{:S(2)}) collective-permute-start(f32[3,2048]{1,0:T(4,128)} %get-tuple-element.113), channel_id=1, source_target_pairs={{1,0},{2,1},{3,2},{5,4},{6,5},{7,6},{9,8},{10,9},{11,10},{13,12},{... | collective-permute-start | bytes 73736 | tf_op jit(solution)/shard_map/ppermute | solution.py:277
  319.1 3.9 copy-start.1
  319.1 4.1 copy-start.10
  319.1 4.3 copy-start.12
  323.4 1.6 copy-start.16
  323.4 2.4 copy-start.35
  325.0 1.8 copy-start.38
  325.0 2.0 copy-start.41
  327.0 3.3 copy-start.5
  330.3 7.0 %copy-start.17 = (bf16[256,2048]{1,0:T(8,128)(2,1)}, bf16[256,2048]{1,0:T(8,128)(2,1)S(1)}, u32[]{:S(2)}) copy-start(bf16[256,2048]{1,0:T(8,128)(2,1)S(1)} %get-tuple-element.216) | copy-start | bytes 3145732
  330.3 3.5 copy-start.19
  333.8 3.5 copy-start.2
  427.9 7.2 %copy-start.25 = (f32[16,8,128]{2,1,0:T(8,128)S(1)}, f32[16,8,128]{2,1,0:T(8,128)}, u32[]{:S(2)}) copy-start(f32[16,8,128]{2,1,0:T(8,128)} %get-tuple-element.134) | copy-start | bytes 196612
  427.9 7.2 %copy-start.26 = (f32[3,2048]{1,0:T(4,128)S(1)}, f32[3,2048]{1,0:T(4,128)}, u32[]{:S(2)}) copy-start(f32[3,2048]{1,0:T(4,128)} %get-tuple-element.129) | copy-start | bytes 73732
  427.9 7.2 %copy-start.39 = (bf16[256,2048]{1,0:T(8,128)(2,1)S(1)}, bf16[256,2048]{1,0:T(8,128)(2,1)}, u32[]{:S(2)}) copy-start(bf16[256,2048]{1,0:T(8,128)(2,1)} %get-tuple-element.128) | copy-start | bytes 3145732
  427.9 7.1 %collective-permute-start.3 = (f32[3,2048]{1,0:T(4,128)}, f32[3,2048]{1,0:T(4,128)S(1)}, u32[]{:S(2)}, u32[]{:S(2)}) collective-permute-start(f32[3,2048]{1,0:T(4,128)} %get-tuple-element.130), channel_id=1, source_target_pairs={{1,0},{2,1},{3,2},{5,4},{6,5},{7,6},{9,8},{10,9},{11,10},{13,12},{... | collective-permute-start | bytes 73736 | tf_op jit(solution)/shard_map/ppermute | solution.py:277
  435.6 3.5 copy-start.21
  439.2 3.4 copy-start.3
  439.2 3.4 copy-start.18
  439.2 3.7 copy-start.34
  442.8 2.0 copy-start.6
  447.2 40.1 %copy-start.22 = (f32[192,128]{1,0:T(8,128)S(1)}, f32[192,128]{1,0:T(8,128)}, u32[]{:S(2)}) copy-start(f32[192,128]{1,0:T(8,128)} %get-tuple-element.140) | copy-start | bytes 294916
  492.2 3.3 copy-start.14
  495.5 2.0 copy-start.4
  497.5 1.4 copy-start.13
where the time goes:
time: 506 us; the launch traced here: 500 us
  Pallas kernels  385 us (76%)
  matrix products  63.2 us (12%)
  local copies, waits for them, and re-layouts  24.6 us (5%)
  starting transfers between devices  10.6 us (2%)
  other arithmetic  10.3 us (2%)
    pallas_call x2, Pallas kernels, backward_scan(): pl.pallas_call(functools.partial(backward_scan_kernel, tasks, counts_of(s...  149 us
    pallas_call x2, Pallas kernels, forward_scan(): pl.pallas_call(functools.partial(forward_scan_kernel, tasks, counts_of(so...  118 us
    pallas_call x1, Pallas kernels, gather_rows(): pl.pallas_call(functools.partial(gather_kernel, tasks, depth, refs_of, le...  56 us
    pallas_call x1, Pallas kernels, reduce_rows(): pl.pallas_call(functools.partial(reduce_kernel, tasks, counts_of(values),...  40.1 us
    dot_general x6, matrix products, outer_sum(): lax.dot_general(left, right, (((0,), (0,)), ((), ())), preferred_element_...  21.2 us
    dot_general x6, matrix products, times_transposed(): lax.dot_general(left, right, (((1,), (1,)), ((), ())), preferred_element_...  18 us
    pallas_call x2, Pallas kernels, conv_grad(): pl.pallas_call(conv_grad_kernel, grid=(inner // width,), in_specs=[cols(c...  12.7 us
    unnamed x92, local copies, waits for them, and re-layouts  12.7 us
  transfers between devices with their start and end apart: 4, of which 2 were waited for; matrix products, arithmetic and copies ran while one was open for 3% of the time, Pallas kernels for 0%

commit v1 on v0

--- a/solution.py
+++ b/solution.py
@@ -143,9 +143,10 @@
         turn = CHUNKS - k if backward else k
         mask = row < CHUNKS - k if backward else row >= k
         ends = [
-            jnp.where(mask, g * pltpu.roll(e, turn, 0) + e, e) for g, e in zip(gains, ends)
+            jnp.where(mask, g, 0.0) * pltpu.roll(e, turn, 0) + e for g, e in zip(gains, ends)
         ]
-        gains = [jnp.where(mask, g * pltpu.roll(g, turn, 0), g) for g in gains]
+        if 2 * k < CHUNKS:
+            gains = [g * pltpu.roll(g, turn, 0) for g in gains]
         total = jnp.where(mask, pltpu.roll(total, turn, 0) + total, total)
         k *= 2
     turn = CHUNKS - 1 if backward else 1

time: 506 us -> 506 us (level)
  no operation moved by 1% of the time
where the time goes in v1:
time: 506 us; the launch traced here: 500 us
  Pallas kernels  385 us (76%)
  matrix products  63.2 us (12%)
  local copies, waits for them, and re-layouts  24.6 us (5%)
  starting transfers between devices  10.6 us (2%)
  other arithmetic  10.3 us (2%)
    pallas_call x2, Pallas kernels, backward_scan(): pl.pallas_call(functools.partial(backward_scan_kernel, tasks, counts_of(s...  150 us
    pallas_call x2, Pallas kernels, forward_scan(): pl.pallas_call(functools.partial(forward_scan_kernel, tasks, counts_of(so...  118 us
    pallas_call x1, Pallas kernels, gather_rows(): pl.pallas_call(functools.partial(gather_kernel, tasks, depth, refs_of, le...  56 us
    pallas_call x1, Pallas kernels, reduce_rows(): pl.pallas_call(functools.partial(reduce_kernel, tasks, counts_of(values),...  39.9 us
    dot_general x6, matrix products, outer_sum(): lax.dot_general(left, right, (((0,), (0,)), ((), ())), preferred_element_...  21.2 us
    dot_general x6, matrix products, times_transposed(): lax.dot_general(left, right, (((1,), (1,)), ((), ())), preferred_element_...  18 us
    pallas_call x2, Pallas kernels, conv_grad(): pl.pallas_call(conv_grad_kernel, grid=(inner // width,), in_specs=[cols(c...  12.7 us
    unnamed x92, local copies, waits for them, and re-layouts  12.7 us
  transfers between devices with their start and end apart: 4, of which 2 were waited for; matrix products, arithmetic and copies ran while one was open for 3% of the time, Pallas kernels for 0%

profile of v1, /device:TPU:0, one launch (start us, length us, event | category | flops | bytes accessed | tf_op | source)
XLA Modules:
  0.0 499.9 jit_solution(13406594872866175891)
XLA Ops:
  0.7 2.1 constant_dynamic-slice_fusion
  3.1 1.2 concatenate.33.refs_3_
  4.2 56.0 %gather_rows.1 = (bf16[2,2,4,2,96,128]{5,4,3,2,1,0:T(8,128)(2,1)}, bf16[2,2,4,2,32,2048]{5,4,3,2,1,0:T(8,128)(2,1)}, bf16[2,2,4,2,32,2048]{5,4,3,2,1,0:T(8,128)(2,1)}) custom-call(bf16[96,128]{1,0:T(8,128)(2,1)} %bitcast.189, bf16[64,128]{1,0:T(8,128)(2,1)} %bitcast.193, bf16[16,128]{1,0:T(8,128)(2,1)} %bitcast.197, bf16[16,128]{1,0:T(8,128)(2,1)} %concatenate.33.refs_3_, ...), custom_call_target="tpu_custom_call" | custom-call | tf_op jit(solution)/shard_map/gather_rows/pallas_call | solution.py:488
  61.3 3.7 convolution_convert_fusion.8.conv_ref
  65.0 1.0 copy-done.7
  66.1 3.3 collective-permute-start
  69.4 1.1 convert_bitcast_fusion
  71.6 4.5 convolution_convert_fusion.7
  76.3 1.0 broadcast_in_dim.29.same_ref
  77.3 4.5 conv_select.2
  82.5 60.3 %forward_scan.2 = (f32[256,2048]{1,0:T(8,128)}, f32[256,2048]{1,0:T(8,128)}, f32[2,2048]{1,0:T(2,128)}, f32[256,2048]{1,0:T(8,128)}, bf16[16,16,272,128]{3,2,1,0...) custom-call(bf16[16,192,128]{2,1,0:T(8,128)(2,1)} %bitcast.154, ...), custom_call_target="tpu_custom_call" | custom-call | tf_op jit(solution)/shard_map/forward_scan/pallas_call | solution.py:1012
  143.7 5.4 %multiply_reduce_fusion.4 = (f32[256]{0:T(256)S(1)}, f32[256,1024]{1,0:T(8,128)S(1)}) fusion(bf16[2048,1024]{1,0:T(8,128)(2,1)} %bitcast.210, f32[256,2048]{1,0:T(8,128)} %get-tuple-element.94, bf16[256,2048]{1,0:T(8,128)(2,1)} %convolution_convert_fusion.7, f32[32,8,1024]{2,0,1:T(8,128)} %convert_bitcast_fusion), kind=kOutput, calls=%fused_computation.52 | convolution fusion | flops 1078198016 | bytes 9438208 | tf_op jit(solution)/shard_map/dot_general | solution.py:1347
  149.2 1.3 convolution_convert_fusion.6.conv_ref
  150.6 1.0 copy-done.8
  151.6 4.6 collective-permute-start.1
  156.2 0.9 collective-permute-done.1.halo_ref
  157.7 4.5 conv_select.3
  162.2 57.3 %forward_scan.3 = (f32[256,2048]{1,0:T(8,128)}, f32[256,2048]{1,0:T(8,128)}, f32[2,2048]{1,0:T(2,128)}, f32[256,2048]{1,0:T(8,128)}, bf16[16,16,272,128]{3,2,1,0...) custom-call(bf16[16,192,128]{2,1,0:T(8,128)(2,1)} %bitcast.159, ...), custom_call_target="tpu_custom_call" | custom-call | tf_op jit(solution)/shard_map/forward_scan/pallas_call | solution.py:1012
  219.5 3.9 fusion.23
  223.8 3.4 fusion.13
  227.2 3.8 convolution_convert_fusion.4
  231.0 3.3 convolution_convert_fusion.3
  234.3 70.0 %backward_scan.2 = (f32[256,2048]{1,0:T(8,128)}, f32[1,2048]{1,0:T(1,128)}, f32[1,2048]{1,0:T(1,128)}, bf16[16,16,128]{2,1,0:T(8,128)(2,1)}, bf16[16,64,128]{2,1...) custom-call(f32[256,2048]{1,0:T(8,128)} %get-tuple-element.219.dfull_ref, ...), custom_call_target="tpu_custom_call" | custom-call | tf_op jit(solution)/shard_map/backward_scan/pallas_call | solution.py:1240
  304.3 6.4 %conv_grad.2 = (bf16[256,2048]{1,0:T(8,128)(2,1)}, f32[3,2048]{1,0:T(4,128)}, f32[3,2048]{1,0:T(4,128)}, bf16[16,96,128]{2,1,0:T(8,128)(2,1)}, f32[16,8,128]{2,1,0:T(8,128)}) custom-call(bf16[256,2048]{1,0:T(8,128)(2,1)} %copy-done.8, bf16[3,2048]{1,0:T(4,128)(2,1)} %copy-done.24, f32[3,256,128]{2,1,0:T(8,128)} %broadcast_in_dim.29.same_ref, ...), custom_call_target="tpu_custom_call" | custom-call | tf_op jit(solution)/shard_map/conv_grad/pallas_call | solution.py:242
  310.7 1.3 collective-permute-start.2
  312.3 0.8 convert.57
  313.2 3.6 collective-permute-done.2
  317.6 1.6 scatter.6
  319.2 3.9 fusion.17
  323.5 1.5 multiply_reduce_fusion.2
  325.9 1.0 copy-done.38
  327.1 3.3 fusion.6
  330.4 3.5 convolution_convert_fusion.2
  333.9 3.3 convolution_convert_fusion.1
  337.4 3.8 convolution_convert_fusion
  341.9 79.8 %backward_scan.3 = (f32[256,2048]{1,0:T(8,128)}, f32[1,2048]{1,0:T(1,128)}, f32[1,2048]{1,0:T(1,128)}, bf16[16,16,128]{2,1,0:T(8,128)(2,1)}, bf16[16,64,128]{2,1...) custom-call(f32[256,2048]{1,0:T(8,128)} %get-tuple-element.217.dfull, ...), custom_call_target="tpu_custom_call", output_to_operand_aliasing={{6}: (15, {}), {7}: (16, {})} | custom-call | tf_op jit(solution)/shard_map/backward_scan/pallas_call | solution.py:1240
  421.7 6.3 %conv_grad.3 = (bf16[256,2048]{1,0:T(8,128)(2,1)}, f32[3,2048]{1,0:T(4,128)}, f32[3,2048]{1,0:T(4,128)}, bf16[16,96,128]{2,1,0:T(8,128)(2,1)}, f32[16,8,128]{2,1,0:T(8,128)}) custom-call(bf16[256,2048]{1,0:T(8,128)(2,1)} %copy-done.7, bf16[3,2048]{1,0:T(4,128)(2,1)} %copy-done.23, f32[3,256,128]{2,1,0:T(8,128)} %broadcast_in_dim.29.same_ref, ...), custom_call_target="tpu_custom_call" | custom-call | tf_op jit(solution)/shard_map/conv_grad/pallas_call | solution.py:242
  428.1 1.4 collective-permute-start.3
  429.5 5.7 %convolution_add_fusion.2.refs_1_ = f32[256,1024]{1,0:T(8,128)} fusion(f32[256,1024]{1,0:T(8,128)} %copy-done, bf16[2048,1024]{1,0:T(8,128)(2,1)} %bitcast.209, f32[256,2048]{1,0:T(8,128)} %get-tuple-element.101, bf16[256,2048]{1,0:T(8,128)(2,1)} %copy-done.42), kind=kOutput, calls=%fused_computation.34 | convolution fusion | flops 1077673984 | bytes 9437184 | tf_op jit(solution)/shard_map/dot_general | solution.py:1347
  435.8 3.5 fusion.14
  439.3 3.4 bitcast_convert_fusion
  443.0 1.9 multiply_reduce_fusion
  445.0 1.6 multiply_add_fusion.refs_2_
  447.3 39.9 %reduce_rows.1 = (f32[2,256,1024]{2,1,0:T(8,128)}, f32[2,256,1024]{2,1,0:T(8,128)}, f32[64,4096]{1,0:T(8,128)}, f32[192,128]{1,0:T(8,128)}) custom-call(f32[256,1024]{1,0:T(8,128)} %copy-done, f32[256,1024]{1,0:T(8,128)} %convolution_add_fusion.2.refs_1_, f32[256,1024]{1,0:T(8,128)} %multiply_add_fusion.refs_2_, ...), custom_call_target="tpu_custom_call", output_to_operand_aliasing={{2}: (9, {})} | custom-call | tf_op jit(solution)/shard_map/reduce_rows/pallas_call | solution.py:790
  487.2 0.9 broadcast_select_fusion
  492.1 3.3 copy.143
  495.4 1.3 copy.144
  497.4 1.0 copy.145
  (153 shorter events, 16.1 us)
Async XLA Ops:
  0.6 2.3 copy-start.40
  0.7 2.4 copy-start.32
  0.7 2.4 copy-start.31
  0.7 2.4 copy-start.30
  0.7 2.4 copy-start.29
  61.3 10.3 %copy-start.20 = (bf16[32,8,1024]{2,0,1:T(8,128)(2,1)}, bf16[32,8,1024]{2,0,1:T(8,128)(2,1)S(1)}, u32[]{:S(2)}) copy-start(bf16[32,8,1024]{2,0,1:T(8,128)(2,1)S(1)} %multiply_convert_fusion.4) | copy-start | bytes 1572868
  61.3 9.3 %copy-start.33 = (s32[2,1,4]{2,1,0:T(1,128)S(1)}, s32[2,1,4]{2,1,0:T(1,128)}, u32[]{:S(2)}) copy-start(s32[2,1,4]{2,1,0:T(1,128)} %param.18) | copy-start | bytes 100
  65.0 1.0 copy-start.7
  66.1 10.2 %collective-permute-start = (bf16[3,2048]{1,0:T(4,128)(2,1)S(1)}, bf16[3,2048]{1,0:T(4,128)(2,1)S(1)}, u32[]{:S(2)}, u32[]{:S(2)}) collective-permute-start(bf16[3,2048]{1,0:T(4,128)(2,1)S(1)} %bitcast.201), channel_id=1, source_target_pairs={{0,1},{1,2},{2,3},{4,5},{5,6},{6,7},{8,9},{9,10},{10,11},{12,13},{... | collective-permute-start | bytes 36872 | tf_op jit(solution)/shard_map/ppermute | solution.py:278
  76.3 1.0 copy-start.23
  143.7 5.6 %copy-start.36 = (bf16[2,2,4,2,32,2048]{5,4,3,2,1,0:T(8,128)(2,1)S(1)}, bf16[2,2,4,2,32,2048]{5,4,3,2,1,0:T(8,128)(2,1)}, u32[]{:S(2)}) copy-start(bf16[2,2,4,2,32,2048]{5,4,3,2,1,0:T(8,128)(2,1)} %get-tuple-element.98) | copy-start | bytes 12582916
  149.0 1.5 copy-start
  150.5 1.0 copy-start.8
  151.6 5.5 %collective-permute-start.1 = (bf16[3,2048]{1,0:T(4,128)(2,1)S(1)}, bf16[3,2048]{1,0:T(4,128)(2,1)S(1)}, u32[]{:S(2)}, u32[]{:S(2)}) collective-permute-start(bf16[3,2048]{1,0:T(4,128)(2,1)S(1)} %bitcast.202), channel_id=1, source_target_pairs={{0,1},{1,2},{2,3},{4,5},{5,6},{6,7},{8,9},{9,10},{10,11},{12,13},{... | collective-permute-start | bytes 36872 | tf_op jit(solution)/shard_map/ppermute | solution.py:278
  157.1 0.6 copy-start.24
  219.5 3.9 copy-start.9
  219.5 4.3 copy-start.37
  223.8 3.4 copy-start.15
  227.2 3.8 copy-start.42
  227.2 3.8 copy-start.11
  304.3 8.0 %copy-start.27 = (f32[2,2048]{1,0:T(2,128)S(1)}, f32[2,2048]{1,0:T(2,128)}, u32[]{:S(2)}) copy-start(f32[2,2048]{1,0:T(2,128)} %get-tuple-element.135) | copy-start | bytes 49156
  304.3 8.0 %copy-start.28 = (f32[2,2048]{1,0:T(2,128)S(1)}, f32[2,2048]{1,0:T(2,128)}, u32[]{:S(2)}) copy-start(f32[2,2048]{1,0:T(2,128)} %get-tuple-element.121) | copy-start | bytes 49156
  310.7 6.0 %collective-permute-start.2 = (f32[3,2048]{1,0:T(4,128)}, f32[3,2048]{1,0:T(4,128)S(1)}, u32[]{:S(2)}, u32[]{:S(2)}) collective-permute-start(f32[3,2048]{1,0:T(4,128)} %get-tuple-element.113), channel_id=1, source_target_pairs={{1,0},{2,1},{3,2},{5,4},{6,5},{7,6},{9,8},{10,9},{11,10},{13,12},{... | collective-permute-start | bytes 73736 | tf_op jit(solution)/shard_map/ppermute | solution.py:278
  319.2 3.9 copy-start.1
  319.2 4.1 copy-start.10
  319.2 4.3 copy-start.12
  323.5 1.6 copy-start.16
  323.5 2.4 copy-start.35
  325.0 1.8 copy-start.38
  325.0 2.0 copy-start.41
  327.1 3.3 copy-start.5
  330.4 7.0 %copy-start.17 = (bf16[256,2048]{1,0:T(8,128)(2,1)}, bf16[256,2048]{1,0:T(8,128)(2,1)S(1)}, u32[]{:S(2)}) copy-start(bf16[256,2048]{1,0:T(8,128)(2,1)S(1)} %get-tuple-element.216) | copy-start | bytes 3145732
  330.4 3.5 copy-start.19
  333.9 3.5 copy-start.2
  428.0 7.2 %copy-start.25 = (f32[16,8,128]{2,1,0:T(8,128)S(1)}, f32[16,8,128]{2,1,0:T(8,128)}, u32[]{:S(2)}) copy-start(f32[16,8,128]{2,1,0:T(8,128)} %get-tuple-element.134) | copy-start | bytes 196612
  428.1 7.2 %copy-start.26 = (f32[3,2048]{1,0:T(4,128)S(1)}, f32[3,2048]{1,0:T(4,128)}, u32[]{:S(2)}) copy-start(f32[3,2048]{1,0:T(4,128)} %get-tuple-element.129) | copy-start | bytes 73732
  428.1 7.2 %copy-start.39 = (bf16[256,2048]{1,0:T(8,128)(2,1)S(1)}, bf16[256,2048]{1,0:T(8,128)(2,1)}, u32[]{:S(2)}) copy-start(bf16[256,2048]{1,0:T(8,128)(2,1)} %get-tuple-element.128) | copy-start | bytes 3145732
  428.1 7.1 %collective-permute-start.3 = (f32[3,2048]{1,0:T(4,128)}, f32[3,2048]{1,0:T(4,128)S(1)}, u32[]{:S(2)}, u32[]{:S(2)}) collective-permute-start(f32[3,2048]{1,0:T(4,128)} %get-tuple-element.130), channel_id=1, source_target_pairs={{1,0},{2,1},{3,2},{5,4},{6,5},{7,6},{9,8},{10,9},{11,10},{13,12},{... | collective-permute-start | bytes 73736 | tf_op jit(solution)/shard_map/ppermute | solution.py:278
  435.7 3.5 copy-start.21
  439.3 3.4 copy-start.3
  439.3 3.4 copy-start.18
  439.3 3.7 copy-start.34
  443.0 2.0 copy-start.6
  447.3 39.9 %copy-start.22 = (f32[192,128]{1,0:T(8,128)S(1)}, f32[192,128]{1,0:T(8,128)}, u32[]{:S(2)}) copy-start(f32[192,128]{1,0:T(8,128)} %get-tuple-element.140) | copy-start | bytes 294916
  492.1 3.3 copy-start.14
  495.4 2.0 copy-start.4
  497.4 1.4 copy-start.13
